TPU v7x, 256 devices: a whole 4x4x8 slice. The times are simulated.
256 devices in a mesh: section: 2 (over y_lo), dp: 16 (over z, y_hi), tensor: 8 (over x, core).
Axes of the slice: x: 4, y: 4 (y_hi: 2, y_lo: 2; y = y_hi * 2 + y_lo), z: 8, core: 2. Of those that a mesh axis runs over, the one named last changes fastest.
Arguments:
- fwd_in: bfloat16 [2, 1024, 8192], P('section', 'tensor', 'dp'), may hold values from -6 to 6
- grad_in: bfloat16 [2, 1024, 8192], P('section', 'tensor', 'dp'), may hold values from -6 to 6
- saved_gate: bfloat16 [2, 1024, 14336], P('section', 'dp', 'tensor'), may hold values from -8 to 8
- saved_up: bfloat16 [2, 1024, 14336], P('section', 'dp', 'tensor'), may hold values from -6 to 6
- gate_weight: bfloat16 [2, 8192, 14336], P('section', 'dp', 'tensor'), may hold values from -0.0625 to 0.0625
- up_weight: bfloat16 [2, 8192, 14336], P('section', 'dp', 'tensor'), may hold values from -0.0625 to 0.0625
- down_weight: bfloat16 [2, 14336, 8192], P('section', 'tensor', 'dp'), may hold values from -0.046875 to 0.046875
Outputs:
- fwd_out: bfloat16 [2, 1024, 8192], P('section', 'tensor', 'dp')
- bwd_out: bfloat16 [2, 1024, 8192], P('section', 'tensor', 'dp')
- handed: bfloat16 [2, 1024, 8192], P('section', 'tensor', 'dp')
All inputs are finite; a program needn't handle non-finite values.
Results may differ from a plain program's by a relative error of at most 0.022.
Values may be sent and summed in bfloat16 or wider, within the bound.
No kernel may reach another device: no remote copies, remote signals or barrier semaphores. Data moves between devices by JAX's collectives and lax.ppermute only.
A program may use at most 128 MiB of HBM per device.

v0:
```python
import jax
import jax.numpy as jnp
from jax import lax
from jax.sharding import PartitionSpec as P


def partner(shard, axis, apart):
    return lax.ppermute(shard, axis, [(i, i ^ 1 << apart) for i in range(lax.axis_size(axis))])


def across_rows(part):
    return lax.all_gather(part, "tensor", axis=0, tiled=True)


def feature_total(term):
    return lax.psum_scatter(term, "tensor", scatter_dimension=0, tiled=True)


def transposed(left, right):
    return lax.dot_general(
        left, right, (((1,), (1,)), ((), ())), preferred_element_type=jnp.float32
    )


def local(fwd_in, grad_in, saved_gate, saved_up, gate_weight, up_weight, down_weight):
    inputs = fwd_in[0]
    grads = grad_in[0]
    w_gate = gate_weight[0]
    w_up = up_weight[0]
    w_down = down_weight[0]
    hidden_cols = w_gate.shape[1]
    all_inputs = across_rows(inputs)
    both = jnp.concatenate(
        [
            jnp.dot(all_inputs, w_gate, preferred_element_type=jnp.float32),
            jnp.dot(all_inputs, w_up, preferred_element_type=jnp.float32),
        ],
        axis=1,
    )
    total = lax.psum(both.astype(jnp.bfloat16), "dp").astype(jnp.float32)
    hidden = (jax.nn.silu(total[:, :hidden_cols]) * total[:, hidden_cols:]).astype(jnp.bfloat16)
    mixed_term = jnp.dot(hidden, w_down, preferred_element_type=jnp.float32)
    mixed = feature_total(mixed_term)
    forward_result = (inputs.astype(jnp.float32) + mixed).astype(jnp.bfloat16)
    all_grads = across_rows(grads)
    slope = lax.psum_scatter(
        transposed(all_grads, w_down).astype(jnp.bfloat16), "dp", scatter_dimension=0, tiled=True
    ).astype(jnp.float32)
    gvals = saved_gate[0].astype(jnp.float32)
    uvals = saved_up[0].astype(jnp.float32)
    sig = jax.nn.sigmoid(gvals)
    gate_grad = (slope * uvals * sig * (1.0 + gvals * (1.0 - sig))).astype(jnp.bfloat16)
    up_grad = (slope * gvals * sig).astype(jnp.bfloat16)
    pieces = lax.all_gather((gate_grad, up_grad), "dp", axis=0, tiled=True)
    back_term = transposed(pieces[0], w_gate) + transposed(pieces[1], w_up)
    back = feature_total(back_term)
    backward_result = (grads.astype(jnp.float32) + back).astype(jnp.bfloat16)
    position = lax.axis_index("section")
    outgoing = jnp.where(position == 0, forward_result, backward_result)
    received = partner(outgoing, "section", 0)
    return (forward_result[None], backward_result[None], received[None])


def solution(mesh):
    placed = (
        P("section", "tensor", "dp"),
        P("section", "tensor", "dp"),
        P("section", "dp", "tensor"),
        P("section", "dp", "tensor"),
        P("section", "dp", "tensor"),
        P("section", "dp", "tensor"),
        P("section", "tensor", "dp"),
    )
    return jax.shard_map(
        local,
        mesh=mesh,
        in_specs=placed,
        out_specs=(
            P("section", "tensor", "dp"),
            P("section", "tensor", "dp"),
            P("section", "tensor", "dp"),
        ),
        check_vma=False,
    )
```

profile of v0, /device:TPU:8, one launch (start us, length us, event | category | flops | bytes accessed | tf_op | source)
XLA Modules:
  0.0 895.1 jit_solution(7980363948949293183)
XLA Ops:
  7.2 0.7 all-gather.13.cloned.1.call-update
  8.0 0.7 all-gather.11.cloned.1.call-update
  8.7 30.0 %all-gather.13.cloned.1.call-done = bf16[1,1024,512]{2,1,0:T(8,128)(2,1)} async-done(((bf16[1,128,512]{2,1,0:T(8,128)(2,1)}), bf16[1,1024,512]{2,1,0:T(8,128)(2,1)}) %all-gather.13.cloned.1.call-update) | async-done | bytes 1048592 | tf_op jit(solution)/shard_map/all_gather | solution.py:12
  38.7 5.2 convolution_convert_fusion
  44.0 22.4 %all-gather.11.cloned.1.call-done = bf16[1,1024,512]{2,1,0:T(8,128)(2,1)} async-done(((bf16[1,128,512]{2,1,0:T(8,128)(2,1)}), bf16[1,1024,512]{2,1,0:T(8,128)(2,1)}) %all-gather.11.cloned.1.call-update) | async-done | bytes 1048592 | tf_op jit(solution)/shard_map/all_gather | solution.py:12
  66.4 5.9 convolution_convert_fusion.1
  72.3 3.9 convolution_convert_fusion.2
  76.2 6.6 pad_maximum_fusion
  82.9 198.7 %reduce-scatter.6.cloned.1.call-done = bf16[64,1792]{1,0:T(8,128)(2,1)} async-done(((bf16[1024,1792]{1,0:T(8,128)(2,1)}), bf16[64,1792]{1,0:T(8,128)(2,1)}) %reduce-scatter.6.cloned.1.call-update) | async-done | bytes 229392 | tf_op jit(solution)/shard_map/reduce_scatter | solution.py:46
  281.6 2.0 fusion.19
  284.3 325.9 %all-reduce.2.cloned.1.call-done = bf16[1024,3584]{1,0:T(8,128)(2,1)} async-done(((bf16[1024,3584]{1,0:T(8,128)(2,1)}), bf16[1024,3584]{1,0:T(8,128)(2,1)}) %all-reduce.2.cloned.1.call-update) | async-done | bytes 7340048 | tf_op jit(solution)/shard_map/psum | solution.py:40
  610.2 10.3 %convert_element_type.44 = f32[1024,3584]{1,0:T(8,128)} convert(bf16[1024,3584]{1,0:T(8,128)(2,1)} %all-reduce.2.cloned.1.call-done) | non-fusion elementwise | flops 3670016 | bytes 22020096 | tf_op jit(solution)/shard_map/convert_element_type | solution.py:40
  620.5 8.6 fusion.1
  629.2 82.3 %all-gather.9.cloned.1.call-done = bf16[1024,1792]{1,0:T(8,128)(2,1)} async-done(((bf16[64,1792]{1,0:T(8,128)(2,1)}), bf16[1024,1792]{1,0:T(8,128)(2,1)}) %all-gather.9.cloned.1.call-update) | async-done | bytes 3670032 | tf_op jit(solution)/shard_map/all_gather | solution.py:54
  711.5 6.0 fusion.5
  717.5 89.9 %all-gather.7.cloned.1.call-done = bf16[1024,1792]{1,0:T(8,128)(2,1)} async-done(((bf16[64,1792]{1,0:T(8,128)(2,1)}), bf16[1024,1792]{1,0:T(8,128)(2,1)}) %all-gather.7.cloned.1.call-update) | async-done | bytes 3670032 | tf_op jit(solution)/shard_map/all_gather | solution.py:54
  807.4 6.7 fusion.11
  814.1 29.6 %reduce-scatter.4.cloned.1.call-done = f32[128,512]{1,0:T(8,128)} async-done(((f32[1024,512]{1,0:T(8,128)}), f32[128,512]{1,0:T(8,128)}) %reduce-scatter.4.cloned.1.call-update) | async-done | bytes 262160 | tf_op jit(solution)/shard_map/reduce_scatter | solution.py:16
  843.7 1.6 fusion.29
  845.3 36.1 %reduce-scatter.8.cloned.1.call-done = f32[128,512]{1,0:T(8,128)} async-done(((f32[1024,512]{1,0:T(8,128)}), f32[128,512]{1,0:T(8,128)}) %reduce-scatter.8.cloned.1.call-update) | async-done | bytes 262160 | tf_op jit(solution)/shard_map/reduce_scatter | solution.py:16
  881.5 1.1 broadcast_select_fusion
  882.6 0.7 collective-permute-start
  883.2 1.6 fusion.30
  884.8 2.8 collective-permute-done
  (29 shorter events, 1.6 us)
Async XLA Ops:
  7.2 31.5 %copy-start = (bf16[1,1792,512]{2,1,0:T(8,128)(2,1)S(1)}, bf16[1,1792,512]{2,1,0:T(8,128)(2,1)}, u32[]{:S(2)}) copy-start(bf16[1,1792,512]{2,1,0:T(8,128)(2,1)} %param.13) | copy-start | bytes 5505028
  7.2 31.5 %all-gather.13.cloned.1.call-start = ((), (), s32[]{:S(2)}) async-start(), calls=%async_computation.10 | async-start | bytes 1179648 | tf_op jit(solution)/shard_map/all_gather | solution.py:12
  7.9 58.4 %all-gather.11.cloned.1.call-start = ((), (), s32[]{:S(2)}) async-start(), calls=%async_computation.9 | async-start | bytes 1179648 | tf_op jit(solution)/shard_map/all_gather | solution.py:12
  8.7 273.0 %reduce-scatter.6.cloned.1.call-start = ((), (), s32[]{:S(2)}) async-start(), calls=%async_computation.5 | async-start | bytes 3899392 | tf_op jit(solution)/shard_map/reduce_scatter | solution.py:46
  43.9 566.3 %all-reduce.2.cloned.1.call-start = ((), (), s32[]{:S(2)}) async-start(), calls=%async_computation.3 | async-start | bytes 14680064 | tf_op jit(solution)/shard_map/psum | solution.py:40
  66.4 5.9 copy-start.5
  66.4 6.0 copy-start.6
  82.8 198.8 %copy-start.3 = (bf16[1,64,1792]{2,1,0:T(8,128)(2,1)S(1)}, bf16[1,64,1792]{2,1,0:T(8,128)(2,1)}, u32[]{:S(2)}) copy-start(bf16[1,64,1792]{2,1,0:T(8,128)(2,1)} %param.10) | copy-start | bytes 688132
  82.8 198.8 %copy-start.4 = (bf16[1,64,1792]{2,1,0:T(8,128)(2,1)S(1)}, bf16[1,64,1792]{2,1,0:T(8,128)(2,1)}, u32[]{:S(2)}) copy-start(bf16[1,64,1792]{2,1,0:T(8,128)(2,1)} %param.9) | copy-start | bytes 688132
  82.8 628.6 %all-gather.9.cloned.1.call-start = ((), (), s32[]{:S(2)}) async-start(), calls=%async_computation.7 | async-start | bytes 3899392 | tf_op jit(solution)/shard_map/all_gather | solution.py:54
  283.7 523.7 %all-gather.7.cloned.1.call-start = ((), (), s32[]{:S(2)}) async-start(), calls=%async_computation.6 | async-start | bytes 3899392 | tf_op jit(solution)/shard_map/all_gather | solution.py:54
  284.2 559.5 %reduce-scatter.4.cloned.1.call-start = ((), (), s32[]{:S(2)}) async-start(), calls=%async_computation.4 | async-start | bytes 2359296 | tf_op jit(solution)/shard_map/reduce_scatter | solution.py:16
  629.1 252.3 %reduce-scatter.8.cloned.1.call-start = ((), (), s32[]{:S(2)}) async-start(), calls=%async_computation.8 | async-start | bytes 2359296 | tf_op jit(solution)/shard_map/reduce_scatter | solution.py:16
  717.5 126.2 %copy-start.1 = (bf16[1,128,512]{2,1,0:T(8,128)(2,1)S(1)}, bf16[1,128,512]{2,1,0:T(8,128)(2,1)}, u32[]{:S(2)}) copy-start(bf16[1,128,512]{2,1,0:T(8,128)(2,1)} %param.7) | copy-start | bytes 393220
  717.5 163.9 %copy-start.2 = (bf16[1,128,512]{2,1,0:T(8,128)(2,1)S(1)}, bf16[1,128,512]{2,1,0:T(8,128)(2,1)}, u32[]{:S(2)}) copy-start(bf16[1,128,512]{2,1,0:T(8,128)(2,1)} %param.8) | copy-start | bytes 393220
  882.6 5.1 collective-permute-start
Sparse Core Ops, SparseCore 0:
  9.9 28.7 all-gather.12
  40.5 25.7 all-gather.10
  70.4 211.2 reduce-scatter.5
  284.4 325.7 all-reduce.1
  613.0 98.4 all-gather.8
  714.3 93.0 all-gather.6
  810.1 33.5 reduce-scatter.3
  846.4 34.9 reduce-scatter.7
where the time goes:
time: 895 us
  waiting for transfers between devices  820 us (92%)
  matrix products  36.3 us (4%)
  other arithmetic  23.3 us (3%)
  between operations  14.2 us (2%)
    psum x1, waiting for transfers between devices, local(): total = lax.psum(both.astype(jnp.bfloat16), 'dp').astype(jnp.float32)  326 us
    reduce_scatter x1, waiting for transfers between devices, local(): lax.psum_scatter(transposed(all_grads, w_down).astype(jnp.bfloat16), 'dp'...  199 us
    all_gather x2, waiting for transfers between devices, local(): pieces = lax.all_gather((gate_grad, up_grad), 'dp', axis=0, tiled=True)  172 us
    reduce_scatter x2, waiting for transfers between devices, feature_total(): return lax.psum_scatter(term, 'tensor', scatter_dimension=0, tiled=True)  65.7 us
    all_gather x2, waiting for transfers between devices, across_rows(): return lax.all_gather(part, 'tensor', axis=0, tiled=True)  52.3 us
    dot_general x3, matrix products, transposed(): lax.dot_general(left, right, (((1,), (1,)), ((), ())), preferred_element_...  17.9 us
  transfers between devices with their start and end apart: 9, of which 9 were waited for; matrix products, arithmetic and copies ran while one was open for 7% of the time, Pallas kernels for 0%

commit v1 on v0

v1 whole, which is shorter than its diff:
```python
import jax
import jax.numpy as jnp
from jax import lax
from jax.sharding import Mesh
from jax.sharding import PartitionSpec as P

F32 = jnp.float32
BF16 = jnp.bfloat16


def shift(v, axis, by):
    n = lax.axis_size(axis)
    return lax.ppermute(v, axis, [(i, (i + by) % n) for i in range(n)])


def part(v, index, size, dim):
    return lax.dynamic_slice_in_dim(v, index * size, size, dim)


def swap_half(v, dim, me):
    size = v.shape[dim] // 2
    kept = part(v, me, size, dim)
    return kept, shift(part(v, 1 - me, size, dim), "y", 1)


def gather_tensor(v):
    chips = jnp.concatenate(
        [v, shift(v, "x", -1), shift(v, "x", 2), shift(v, "x", 1)], axis=0
    )
    return jnp.concatenate([chips, shift(chips, "c", 1)], axis=0)


def reduce_tensor(v):
    half = v.shape[0] // 2
    rows = half // 4
    v = v[:half] + shift(v[half:].astype(BF16), "c", 1).astype(F32)
    block = [v[j * rows:(j + 1) * rows] for j in range(4)]
    total = block[0]
    for j, by in ((1, 1), (3, -1), (2, 2)):
        total = total + shift(block[j].astype(BF16), "x", by).astype(F32)
    return total


def ring_reduce(block, width):
    def add(left, right):
        return (left.astype(F32) + right.astype(F32)).astype(BF16)

    half = width // 2
    far = block(4)
    up, down = shift(far[:, :half], "z", 1), shift(far[:, half:], "z", -1)
    a, b = block(3), block(-3)
    up = jnp.concatenate([add(a[:, :half], up), a[:, half:]], axis=1)
    down = jnp.concatenate([b[:, :half], add(b[:, half:], down)], axis=1)
    up, down = shift(up, "z", 1), shift(down, "z", -1)
    up, down = shift(add(block(2), up), "z", 1), shift(add(block(-2), down), "z", -1)
    up, down = shift(add(block(1), up), "z", 1), shift(add(block(-1), down), "z", -1)
    return block(0).astype(F32) + up.astype(F32) + down.astype(F32)


def ring_gather(v):
    half = v.shape[1] // 2
    a1, b1 = shift(v, "z", -1), shift(v, "z", 1)
    a2, b2 = shift(a1, "z", -1), shift(b1, "z", 1)
    a3, b3 = shift(a2, "z", -1), shift(b2, "z", 1)
    a4, b4 = shift(a3[:, :half], "z", -1), shift(b3[:, half:], "z", 1)
    return [v, a1, a2, a3, jnp.concatenate([a4, b4], axis=1), b3, b2, b1]


def local(fwd_in, grad_in, saved_gate, saved_up, gate_weight, up_weight, down_weight):
    inputs = fwd_in[0]
    grads = grad_in[0]
    z, y = lax.axis_index("z"), lax.axis_index("y")
    x, c = lax.axis_index("x"), lax.axis_index("c")
    rows, feats = inputs.shape

    def place(k):
        owner = (z + k) % 8
        return 4 * ((owner % 2 + c) % 2) + (owner // 2 + 4 - x) % 4

    grads_pair = jnp.concatenate([grads, shift(grads, "y", 1)], axis=1)
    kept, got = swap_half(down_weight[0], 0, y)
    w_down = jnp.concatenate([kept, got], axis=1)
    inputs_pair = jnp.concatenate([inputs, shift(inputs, "y", 1)], axis=1)
    cols = w_down.shape[0]
    w_both = jnp.stack([gate_weight[0], up_weight[0]])
    kept, got = swap_half(w_both, 2, y)
    w_both = jnp.concatenate(
        [jnp.concatenate([kept[0], kept[1]], axis=1), jnp.concatenate([got[0], got[1]], axis=1)],
        axis=0,
    )
    kept, got = swap_half(jnp.stack([saved_gate[0], saved_up[0]]), 2, y)
    saved = jnp.where(
        y == 0, jnp.concatenate([kept, got], axis=1), jnp.concatenate([got, kept], axis=1)
    ).astype(F32)

    all_grads = gather_tensor(grads_pair)
    all_inputs = gather_tensor(inputs_pair)

    term = lax.dot_general(
        all_grads, w_down, (((1,), (1,)), ((), ())), preferred_element_type=F32
    ).astype(BF16)
    slope = ring_reduce(lambda k: part(term, place(k), rows, 0), cols)

    both = jnp.dot(all_inputs, w_both, preferred_element_type=F32).astype(BF16)
    both = lax.psum_scatter(both, "z", scatter_dimension=0, tiled=True).astype(F32)
    hidden = (jax.nn.silu(both[:, :cols]) * both[:, cols:]).astype(BF16)
    hidden = lax.all_gather(hidden, "z", axis=0, tiled=True)

    gvals, uvals = saved[0], saved[1]
    sig = jax.nn.sigmoid(gvals)
    gate_grad = (slope * uvals * sig * (1.0 + gvals * (1.0 - sig))).astype(BF16)
    up_grad = (slope * gvals * sig).astype(BF16)
    pieces = jnp.zeros((8 * rows, 2 * cols), BF16)
    for k, piece in enumerate(ring_gather(jnp.concatenate([gate_grad, up_grad], axis=1))):
        pieces = lax.dynamic_update_slice_in_dim(pieces, piece, place(k) * rows, 0)
    back = lax.dot_general(pieces, w_both, (((1,), (1,)), ((), ())), preferred_element_type=F32)
    back = reduce_tensor(back)
    back = back[:, :feats] + shift(back[:, feats:].astype(BF16), "y", 1).astype(F32)
    backward_result = (grads.astype(F32) + back).astype(BF16)

    mixed = jnp.dot(hidden, w_down, preferred_element_type=F32)
    mixed = reduce_tensor(mixed)
    mixed = mixed[:, :feats] + shift(mixed[:, feats:].astype(BF16), "y", 1).astype(F32)
    forward_result = (inputs.astype(F32) + mixed).astype(BF16)

    outgoing = jnp.where(lax.axis_index("s") == 0, forward_result, backward_result)
    received = shift(outgoing, "s", 1)
    return (forward_result[None], backward_result[None], received[None])


def solution(mesh):
    fine = Mesh(mesh.devices.reshape(2, 8, 2, 4, 2), ("s", "z", "y", "x", "c"))
    tokens = P("s", ("x", "c"), ("z", "y"))
    hidden = P("s", ("z", "y"), ("x", "c"))
    return jax.shard_map(
        local,
        mesh=fine,
        in_specs=(tokens, tokens, hidden, hidden, hidden, hidden, tokens),
        out_specs=(tokens, tokens, tokens),
        check_vma=False,
    )
```

time: 895 us -> 307 us (0.34)
  waiting for transfers between devices: 820 us -> 148 us
  starting transfers between devices: 0.98 us -> 58.3 us
  local copies, waits for them, and re-layouts: 0.69 us -> 34.5 us
  other arithmetic: 23.3 us -> 14.3 us
    psum x1 -> x0, waiting for transfers between devices: 326 us -> none  [local(): total = lax.psum(both.astype(jnp.bfloat16), 'dp').astype(jnp.float32)]
    reduce_scatter x3 -> x1, waiting for transfers between devices: 264 us -> 0.01 us  [local(): lax.psum_scatter(both, 'z', scatter_dimension=0, tiled=True).astype(F32)]
    all_gather x4 -> x1, waiting for transfers between devices: 225 us -> 0.02 us  [local(): hidden = lax.all_gather(hidden, 'z', axis=0, tiled=True)]
    ppermute x1 -> x40, waiting for transfers between devices: 2.76 us -> 148 us  [shift(): return lax.ppermute(v, axis, [(i, (i + by) % n) for i in range(n)])]
    ppermute x1 -> x40, starting transfers between devices: 0.66 us -> 58.2 us  [shift(): return lax.ppermute(v, axis, [(i, (i + by) % n) for i in range(n)])]
    unnamed x15 -> x53, local copies, waits for them, and re-layouts: 0.69 us -> 13.9 us
    dot_general x6 -> x4, matrix products: 36.3 us -> 32.1 us  [the longest x1 17.7 us: local(): both = jnp.dot(all_inputs, w_both, preferred_element_type=F32).astype(BF16)]
  transfers between devices with their start and end apart: 9 -> 42, of which waited for: 9 -> 30; matrix products, arithmetic and copies ran while one was open for 7% -> 19% of each run, Pallas kernels for 0% -> 0%
where the time goes in v1:
time: 307 us; the launch traced here: 302 us
  waiting for transfers between devices  148 us (48%)
  starting transfers between devices  58.3 us (19%)
  local copies, waits for them, and re-layouts  34.5 us (11%)
  matrix products  32.1 us (10%)
  between operations  15 us (5%)
  other arithmetic  14.3 us (5%)
    ppermute x40, waiting for transfers between devices, shift(): return lax.ppermute(v, axis, [(i, (i + by) % n) for i in range(n)])  148 us
    ppermute x40, starting transfers between devices, shift(): return lax.ppermute(v, axis, [(i, (i + by) % n) for i in range(n)])  58.2 us
    dot_general x1, matrix products, local(): both = jnp.dot(all_inputs, w_both, preferred_element_type=F32).astype(BF16)  17.7 us
    unnamed x53, local copies, waits for them, and re-layouts  13.9 us
  transfers between devices with their start and end apart: 42, of which 30 were waited for; matrix products, arithmetic and copies ran while one was open for 19% of the time, Pallas kernels for 0%

profile of v1, /device:TPU:8, one launch (start us, length us, event | category | flops | bytes accessed | tf_op | source)
XLA Modules:
  0.0 302.0 jit_solution(15242646652012105566)
XLA Ops:
  23.9 5.7 %collective-permute-done.2 = bf16[128,1024]{1,0:T(8,128)(2,1)S(1)} collective-permute-done((bf16[128,1024]{1,0:T(8,128)(2,1)S(1)}, bf16[128,1024]{1,0:T(8,128)(2,1)S(1)}, u32[]{:S(2)}, u32[]{:S(2)}) %collective-permute-start.2) | collective-permute-done | bytes 262176 | tf_op jit(solution)/shard_map/ppermute | solution.py:13
  29.6 4.0 %collective-permute-done.1 = bf16[128,1024]{1,0:T(8,128)(2,1)S(1)} collective-permute-done((bf16[128,1024]{1,0:T(8,128)(2,1)S(1)}, bf16[128,1024]{1,0:T(8,128)(2,1)S(1)}, u32[]{:S(2)}, u32[]{:S(2)}) %collective-permute-start.1) | collective-permute-done | bytes 262176 | tf_op jit(solution)/shard_map/ppermute | solution.py:13
  38.8 21.3 %collective-permute-done.5 = bf16[2,512,896]{2,1,0:T(8,128)(2,1)S(1)} collective-permute-done((bf16[2,512,896]{2,1,0:T(8,128)(2,1)}, bf16[2,512,896]{2,1,0:T(8,128)(2,1)S(1)}, u32[]{:S(2)}, u32[]{:S(2)}) %collective-permute-start.5) | collective-permute-done | bytes 1835040 | tf_op jit(solution)/shard_map/ppermute | solution.py:13
  61.4 17.7 %convolution_convert_fusion = bf16[1024,1792]{1,0:T(8,128)(2,1)} fusion(bf16[1024,1024]{1,0:T(8,128)(2,1)S(1)} %constant_dynamic-update-slice_fusion, bf16[512,896]{1,0:T(8,128)(2,1)S(1)} %get-tuple-element.15, bf16[512,896]{1,0:T(8,128)(2,1)S(1)} %get-tuple-element.14, bf16[512,896]{1,0:T(8,128)(2,1)S(1)} %get-tuple-element.11, ...), kind=kOutput, calls=%fused_computation | convolution fusion | flops 3774611456 | bytes 9437184 | tf_op jit(solution)/shard_map/dot_general | solution.py:104
  81.2 5.2 %collective-permute-done.12 = bf16[128,512]{1,0:T(8,128)(2,1)S(1)} collective-permute-done((bf16[128,512]{1,0:T(8,128)(2,1)S(1)}, bf16[128,512]{1,0:T(8,128)(2,1)S(1)}, u32[]{:S(2)}, u32[]{:S(2)}) %collective-permute-start.12) | collective-permute-done | bytes 131104 | tf_op jit(solution)/shard_map/ppermute | solution.py:13
  92.3 5.1 %collective-permute-done.14 = bf16[128,1024]{1,0:T(8,128)(2,1)S(1)} collective-permute-done((bf16[128,1024]{1,0:T(8,128)(2,1)S(1)}, bf16[128,1024]{1,0:T(8,128)(2,1)S(1)}, u32[]{:S(2)}, u32[]{:S(2)}) %collective-permute-start.14) | collective-permute-done | bytes 262176 | tf_op jit(solution)/shard_map/ppermute | solution.py:13
  110.3 17.0 %collective-permute-done.6 = bf16[896,512]{1,0:T(8,128)(2,1)} collective-permute-done((bf16[896,512]{1,0:T(8,128)(2,1)}, bf16[896,512]{1,0:T(8,128)(2,1)}, u32[]{:S(2)}, u32[]{:S(2)}) %collective-permute-start.6) | collective-permute-done | bytes 917536 | tf_op jit(solution)/shard_map/ppermute | solution.py:13
  127.3 4.2 %convolution_convert_fusion.1 = bf16[1024,896]{1,0:T(8,128)(2,1)S(1)} fusion(bf16[1024,1024]{1,0:T(8,128)(2,1)} %constant_dynamic-update-slice_fusion.7, bf16[896,512]{1,0:T(8,128)(2,1)} %collective-permute-done.6, bf16[896,512]{1,0:T(8,128)(2,1)S(1)} %copy-done.20), kind=kOutput, calls=%fused_computation.7 | convolution fusion | flops 1883635712 | bytes 5767168 | tf_op jit(solution)/shard_map/dot_general | solution.py:99
  133.7 4.0 %collective-permute-start.21 = (bf16[128,448]{1,0:T(8,128)(2,1)S(1)}, bf16[128,448]{1,0:T(8,128)(2,1)S(1)}, u32[]{:S(2)}, u32[]{:S(2)}) collective-permute-start(bf16[128,448]{1,0:T(8,128)(2,1)S(1)} %get-tuple-element.22), channel_id=1, source_target_pairs={{0,112},{16,0},{32,16},{48,32},{64,48},{80,64},{96,80},{112,96},{1... | collective-permute-start | bytes 344072 | tf_op jit(solution)/shard_map/ppermute | solution.py:13
  145.3 4.7 %collective-permute-done.18 = bf16[128,896]{1,0:T(8,128)(2,1)} collective-permute-done((bf16[128,896]{1,0:T(8,128)(2,1)}, bf16[128,896]{1,0:T(8,128)(2,1)}, u32[]{:S(2)}, u32[]{:S(2)}) %collective-permute-start.18) | collective-permute-done | bytes 229408 | tf_op jit(solution)/shard_map/ppermute | solution.py:13
  152.0 6.2 %collective-permute-done.19 = bf16[128,896]{1,0:T(8,128)(2,1)S(1)} collective-permute-done((bf16[128,896]{1,0:T(8,128)(2,1)S(1)}, bf16[128,896]{1,0:T(8,128)(2,1)S(1)}, u32[]{:S(2)}, u32[]{:S(2)}) %collective-permute-start.19) | collective-permute-done | bytes 229408 | tf_op jit(solution)/shard_map/ppermute | solution.py:13
  170.2 3.4 %collective-permute-done.24 = bf16[128,896]{1,0:T(8,128)(2,1)} collective-permute-done((bf16[128,896]{1,0:T(8,128)(2,1)}, bf16[128,896]{1,0:T(8,128)(2,1)}, u32[]{:S(2)}, u32[]{:S(2)}) %collective-permute-start.24) | collective-permute-done | bytes 229408 | tf_op jit(solution)/shard_map/ppermute | solution.py:13
  180.7 8.8 %collective-permute-done.26 = bf16[128,1792]{1,0:T(8,128)(2,1)S(1)} collective-permute-done((bf16[128,1792]{1,0:T(8,128)(2,1)S(1)}, bf16[128,1792]{1,0:T(8,128)(2,1)S(1)}, u32[]{:S(2)}, u32[]{:S(2)}) %collective-permute-start.26) | collective-permute-done | bytes 458784 | tf_op jit(solution)/shard_map/ppermute | solution.py:13
  195.4 7.1 %collective-permute-done.27 = bf16[128,1792]{1,0:T(8,128)(2,1)S(1)} collective-permute-done((bf16[128,1792]{1,0:T(8,128)(2,1)S(1)}, bf16[128,1792]{1,0:T(8,128)(2,1)S(1)}, u32[]{:S(2)}, u32[]{:S(2)}) %collective-permute-start.27) | collective-permute-done | bytes 458784 | tf_op jit(solution)/shard_map/ppermute | solution.py:13
  202.4 3.7 %collective-permute-start.28 = (bf16[128,1792]{1,0:T(8,128)(2,1)S(1)}, bf16[128,1792]{1,0:T(8,128)(2,1)S(1)}, u32[]{:S(2)}, u32[]{:S(2)}) collective-permute-start(bf16[128,1792]{1,0:T(8,128)(2,1)S(1)} %collective-permute-done.27), channel_id=1, source_target_pairs={{0,112},{16,0},{32,16},{48,32},{64,48},{80,64},{96,80},{112,96},{1... | collective-permute-start | bytes 1376264 | tf_op jit(solution)/shard_map/ppermute | solution.py:13
  208.5 12.2 %collective-permute-done.28 = bf16[128,1792]{1,0:T(8,128)(2,1)S(1)} collective-permute-done((bf16[128,1792]{1,0:T(8,128)(2,1)S(1)}, bf16[128,1792]{1,0:T(8,128)(2,1)S(1)}, u32[]{:S(2)}, u32[]{:S(2)}) %collective-permute-start.28) | collective-permute-done | bytes 458784 | tf_op jit(solution)/shard_map/ppermute | solution.py:13
  227.4 4.5 %collective-permute-done.29 = bf16[128,896]{1,0:T(8,128)(2,1)S(1)} collective-permute-done((bf16[128,896]{1,0:T(8,128)(2,1)S(1)}, bf16[128,896]{1,0:T(8,128)(2,1)S(1)}, u32[]{:S(2)}, u32[]{:S(2)}) %collective-permute-start.29) | collective-permute-done | bytes 229408 | tf_op jit(solution)/shard_map/ppermute | solution.py:13
  231.9 5.6 %collective-permute-done.33 = bf16[128,896]{1,0:T(8,128)(2,1)S(1)} collective-permute-done((bf16[128,896]{1,0:T(8,128)(2,1)S(1)}, bf16[128,896]{1,0:T(8,128)(2,1)S(1)}, u32[]{:S(2)}, u32[]{:S(2)}) %collective-permute-start.33) | collective-permute-done | bytes 229408 | tf_op jit(solution)/shard_map/ppermute | solution.py:13
  240.8 6.0 %fusion.1 = f32[1024,1024]{1,0:T(8,128)S(1)} fusion(bf16[1024,1792]{1,0:T(8,128)(2,1)} %constant_dynamic-update-slice_fusion.14, bf16[512,896]{1,0:T(8,128)(2,1)S(1)} %copy-done.15, bf16[512,896]{1,0:T(8,128)(2,1)S(1)} %copy-done.13, bf16[512,896]{1,0:T(8,128)(2,1)S(1)} %copy-done.19, bf16[512,896]{1,0:T(8,128)(2,1)S(1)} %copy-done.17), kind=kOutput, calls=%fused_computation.17 | convolution fusion | flops 3772776448 | bytes 11534336 | tf_op jit(solution)/shard_map/dot_general | solution.py:116
  249.1 4.2 %fusion = f32[1024,1024]{1,0:T(8,128)S(1)} fusion(bf16[1024,896]{1,0:T(8,128)(2,1)} %all-gather.2.cloned.1.call-done, bf16[896,512]{1,0:T(8,128)(2,1)} %collective-permute-done.6, bf16[896,512]{1,0:T(8,128)(2,1)S(1)} %copy-done.20), kind=kOutput, calls=%fused_computation.8 | convolution fusion | flops 1882718208 | bytes 7864320 | tf_op jit(solution)/shard_map/dot_general | solution.py:121
  266.3 5.1 %collective-permute-done.37 = bf16[128,1024]{1,0:T(8,128)(2,1)S(1)} collective-permute-done((bf16[128,1024]{1,0:T(8,128)(2,1)S(1)}, bf16[128,1024]{1,0:T(8,128)(2,1)S(1)}, u32[]{:S(2)}, u32[]{:S(2)}) %collective-permute-start.37) | collective-permute-done | bytes 262176 | tf_op jit(solution)/shard_map/ppermute | solution.py:13
  275.7 6.0 %collective-permute-done.10 = bf16[128,1024]{1,0:T(8,128)(2,1)S(1)} collective-permute-done((bf16[128,1024]{1,0:T(8,128)(2,1)S(1)}, bf16[128,1024]{1,0:T(8,128)(2,1)S(1)}, u32[]{:S(2)}, u32[]{:S(2)}) %collective-permute-start.10) | collective-permute-done | bytes 262176 | tf_op jit(solution)/shard_map/ppermute | solution.py:13
  284.3 4.1 %collective-permute-done.11 = bf16[128,512]{1,0:T(8,128)(2,1)S(1)} collective-permute-done((bf16[128,512]{1,0:T(8,128)(2,1)S(1)}, bf16[128,512]{1,0:T(8,128)(2,1)S(1)}, u32[]{:S(2)}, u32[]{:S(2)}) %collective-permute-start.11) | collective-permute-done | bytes 131104 | tf_op jit(solution)/shard_map/ppermute | solution.py:13
  290.2 4.1 %collective-permute-done.39 = bf16[128,512]{1,0:T(8,128)(2,1)S(1)} collective-permute-done((bf16[128,512]{1,0:T(8,128)(2,1)S(1)}, bf16[128,512]{1,0:T(8,128)(2,1)S(1)}, u32[]{:S(2)}, u32[]{:S(2)}) %collective-permute-start.39) | collective-permute-done | bytes 131104 | tf_op jit(solution)/shard_map/ppermute | solution.py:13
  (165 shorter events, 117.2 us)
Async XLA Ops:
  7.2 186.0 %reduce-scatter.2.cloned.1.call-start = ((), (), s32[]{:S(2)}) async-start(), calls=%async_computation.1 | async-start | bytes 4128768 | tf_op jit(solution)/shard_map/reduce_scatter | solution.py:105
  7.2 10.9 %collective-permute-start = (bf16[128,512]{1,0:T(8,128)(2,1)}, bf16[128,512]{1,0:T(8,128)(2,1)S(1)}, u32[]{:S(2)}, u32[]{:S(2)}) collective-permute-start(bf16[128,512]{1,0:T(8,128)(2,1)} %bitcast.44), channel_id=1, source_target_pairs={{0,8},{8,0},{1,9},{9,1},{2,10},{10,2},{3,11},{11,3},{4,12},{12,4},... | collective-permute-start | bytes 393224 | tf_op jit(solution)/shard_map/ppermute | solution.py:13
  16.8 43.2 %collective-permute-start.5 = (bf16[2,512,896]{2,1,0:T(8,128)(2,1)}, bf16[2,512,896]{2,1,0:T(8,128)(2,1)S(1)}, u32[]{:S(2)}, u32[]{:S(2)}) collective-permute-start(bf16[2,512,896]{2,1,0:T(8,128)(2,1)} %constant_dynamic-slice_fusion.4), channel_id=1, source_target_pairs={{0,8},{8,0},{1,9},{9,1},{2,10},{10,2},{3,11},{11,3},{4,12},{12,4},... | collective-permute-start | bytes 5505032 | tf_op jit(solution)/shard_map/ppermute | solution.py:13
  18.8 10.8 %collective-permute-start.2 = (bf16[128,1024]{1,0:T(8,128)(2,1)S(1)}, bf16[128,1024]{1,0:T(8,128)(2,1)S(1)}, u32[]{:S(2)}, u32[]{:S(2)}) collective-permute-start(bf16[128,1024]{1,0:T(8,128)(2,1)S(1)} %get-tuple-element.36), channel_id=1, source_target_pairs={{0,4},{2,6},{4,0},{6,2},{1,5},{3,7},{5,1},{7,3},{8,12},{10,14},{12... | collective-permute-start | bytes 786440 | tf_op jit(solution)/shard_map/ppermute | solution.py:13
  21.9 11.7 %collective-permute-start.1 = (bf16[128,1024]{1,0:T(8,128)(2,1)S(1)}, bf16[128,1024]{1,0:T(8,128)(2,1)S(1)}, u32[]{:S(2)}, u32[]{:S(2)}) collective-permute-start(bf16[128,1024]{1,0:T(8,128)(2,1)S(1)} %get-tuple-element.36), channel_id=1, source_target_pairs={{0,6},{2,0},{4,2},{6,4},{1,7},{3,1},{5,3},{7,5},{8,14},{10,8},{12,... | collective-permute-start | bytes 786440 | tf_op jit(solution)/shard_map/ppermute | solution.py:13
  23.0 10.6 %collective-permute-start.3 = (bf16[128,1024]{1,0:T(8,128)(2,1)S(1)}, bf16[128,1024]{1,0:T(8,128)(2,1)S(1)}, u32[]{:S(2)}, u32[]{:S(2)}) collective-permute-start(bf16[128,1024]{1,0:T(8,128)(2,1)S(1)} %get-tuple-element.36), channel_id=1, source_target_pairs={{0,2},{2,4},{4,6},{6,0},{1,3},{3,5},{5,7},{7,1},{8,10},{10,12},{12... | collective-permute-start | bytes 786440 | tf_op jit(solution)/shard_map/ppermute | solution.py:13
  79.1 170.0 %all-gather.2.cloned.1.call-start = ((), (), s32[]{:S(2)}) async-start(), calls=%async_computation.2 | async-start | bytes 2064384 | tf_op jit(solution)/shard_map/all_gather | solution.py:107
  87.2 10.1 %collective-permute-start.14 = (bf16[128,1024]{1,0:T(8,128)(2,1)S(1)}, bf16[128,1024]{1,0:T(8,128)(2,1)S(1)}, u32[]{:S(2)}, u32[]{:S(2)}) collective-permute-start(bf16[128,1024]{1,0:T(8,128)(2,1)S(1)} %get-tuple-element.38), channel_id=1, source_target_pairs={{0,4},{2,6},{4,0},{6,2},{1,5},{3,7},{5,1},{7,3},{8,12},{10,14},{12... | collective-permute-start | bytes 786440 | tf_op jit(solution)/shard_map/ppermute | solution.py:13
  102.6 24.6 %collective-permute-start.6 = (bf16[896,512]{1,0:T(8,128)(2,1)}, bf16[896,512]{1,0:T(8,128)(2,1)}, u32[]{:S(2)}, u32[]{:S(2)}) collective-permute-start(bf16[896,512]{1,0:T(8,128)(2,1)} %get-tuple-element.25), channel_id=1, source_target_pairs={{0,8},{8,0},{1,9},{9,1},{2,10},{10,2},{3,11},{11,3},{4,12},{12,4},... | collective-permute-start | bytes 2752520 | tf_op jit(solution)/shard_map/ppermute | solution.py:13
  177.8 11.7 %collective-permute-start.26 = (bf16[128,1792]{1,0:T(8,128)(2,1)S(1)}, bf16[128,1792]{1,0:T(8,128)(2,1)S(1)}, u32[]{:S(2)}, u32[]{:S(2)}) collective-permute-start(bf16[128,1792]{1,0:T(8,128)(2,1)S(1)} %get-tuple-element.32), channel_id=1, source_target_pairs={{0,112},{16,0},{32,16},{48,32},{64,48},{80,64},{96,80},{112,96},{1... | collective-permute-start | bytes 1376264 | tf_op jit(solution)/shard_map/ppermute | solution.py:13
  180.5 12.7 %collective-permute-start.30 = (bf16[128,1792]{1,0:T(8,128)(2,1)S(1)}, bf16[128,1792]{1,0:T(8,128)(2,1)S(1)}, u32[]{:S(2)}, u32[]{:S(2)}) collective-permute-start(bf16[128,1792]{1,0:T(8,128)(2,1)S(1)} %get-tuple-element.32), channel_id=1, source_target_pairs={{0,16},{16,32},{32,48},{48,64},{64,80},{80,96},{96,112},{112,0},{1... | collective-permute-start | bytes 1376264 | tf_op jit(solution)/shard_map/ppermute | solution.py:13
  189.5 13.0 %collective-permute-start.27 = (bf16[128,1792]{1,0:T(8,128)(2,1)S(1)}, bf16[128,1792]{1,0:T(8,128)(2,1)S(1)}, u32[]{:S(2)}, u32[]{:S(2)}) collective-permute-start(bf16[128,1792]{1,0:T(8,128)(2,1)S(1)} %collective-permute-done.26), channel_id=1, source_target_pairs={{0,112},{16,0},{32,16},{48,32},{64,48},{80,64},{96,80},{112,96},{1... | collective-permute-start | bytes 1376264 | tf_op jit(solution)/shard_map/ppermute | solution.py:13
  193.2 13.7 %collective-permute-start.31 = (bf16[128,1792]{1,0:T(8,128)(2,1)S(1)}, bf16[128,1792]{1,0:T(8,128)(2,1)S(1)}, u32[]{:S(2)}, u32[]{:S(2)}) collective-permute-start(bf16[128,1792]{1,0:T(8,128)(2,1)S(1)} %collective-permute-done.30), channel_id=1, source_target_pairs={{0,16},{16,32},{32,48},{48,64},{64,80},{80,96},{96,112},{112,0},{1... | collective-permute-start | bytes 1376264 | tf_op jit(solution)/shard_map/ppermute | solution.py:13
  202.4 18.3 %collective-permute-start.28 = (bf16[128,1792]{1,0:T(8,128)(2,1)S(1)}, bf16[128,1792]{1,0:T(8,128)(2,1)S(1)}, u32[]{:S(2)}, u32[]{:S(2)}) collective-permute-start(bf16[128,1792]{1,0:T(8,128)(2,1)S(1)} %collective-permute-done.27), channel_id=1, source_target_pairs={{0,112},{16,0},{32,16},{48,32},{64,48},{80,64},{96,80},{112,96},{1... | collective-permute-start | bytes 1376264 | tf_op jit(solution)/shard_map/ppermute | solution.py:13
  206.9 19.6 %collective-permute-start.32 = (bf16[128,1792]{1,0:T(8,128)(2,1)S(1)}, bf16[128,1792]{1,0:T(8,128)(2,1)S(1)}, u32[]{:S(2)}, u32[]{:S(2)}) collective-permute-start(bf16[128,1792]{1,0:T(8,128)(2,1)S(1)} %collective-permute-done.31), channel_id=1, source_target_pairs={{0,16},{16,32},{32,48},{48,64},{64,80},{80,96},{96,112},{112,0},{1... | collective-permute-start | bytes 1376264 | tf_op jit(solution)/shard_map/ppermute | solution.py:13
  220.8 11.2 %collective-permute-start.29 = (bf16[128,896]{1,0:T(8,128)(2,1)S(1)}, bf16[128,896]{1,0:T(8,128)(2,1)S(1)}, u32[]{:S(2)}, u32[]{:S(2)}) collective-permute-start(bf16[128,896]{1,0:T(8,128)(2,1)S(1)} %slice.152), channel_id=1, source_target_pairs={{0,112},{16,0},{32,16},{48,32},{64,48},{80,64},{96,80},{112,96},{1... | collective-permute-start | bytes 688136 | tf_op jit(solution)/shard_map/ppermute | solution.py:13
  226.5 11.0 %collective-permute-start.33 = (bf16[128,896]{1,0:T(8,128)(2,1)S(1)}, bf16[128,896]{1,0:T(8,128)(2,1)S(1)}, u32[]{:S(2)}, u32[]{:S(2)}) collective-permute-start(bf16[128,896]{1,0:T(8,128)(2,1)S(1)} %slice.153), channel_id=1, source_target_pairs={{0,16},{16,32},{32,48},{48,64},{64,80},{80,96},{96,112},{112,0},{1... | collective-permute-start | bytes 688136 | tf_op jit(solution)/shard_map/ppermute | solution.py:13
  254.7 10.8 %collective-permute-start.35 = (bf16[128,1024]{1,0:T(8,128)(2,1)S(1)}, bf16[128,1024]{1,0:T(8,128)(2,1)S(1)}, u32[]{:S(2)}, u32[]{:S(2)}) collective-permute-start(bf16[128,1024]{1,0:T(8,128)(2,1)S(1)} %get-tuple-element.29), channel_id=1, source_target_pairs={{0,2},{2,4},{4,6},{6,0},{1,3},{3,5},{5,7},{7,1},{8,10},{10,12},{12... | collective-permute-start | bytes 786440 | tf_op jit(solution)/shard_map/ppermute | solution.py:13
  255.6 15.8 %collective-permute-start.37 = (bf16[128,1024]{1,0:T(8,128)(2,1)S(1)}, bf16[128,1024]{1,0:T(8,128)(2,1)S(1)}, u32[]{:S(2)}, u32[]{:S(2)}) collective-permute-start(bf16[128,1024]{1,0:T(8,128)(2,1)S(1)} %get-tuple-element.30), channel_id=1, source_target_pairs={{0,4},{2,6},{4,0},{6,2},{1,5},{3,7},{5,1},{7,3},{8,12},{10,14},{12... | collective-permute-start | bytes 786440 | tf_op jit(solution)/shard_map/ppermute | solution.py:13
  258.6 13.1 %collective-permute-start.36 = (bf16[128,1024]{1,0:T(8,128)(2,1)S(1)}, bf16[128,1024]{1,0:T(8,128)(2,1)S(1)}, u32[]{:S(2)}, u32[]{:S(2)}) collective-permute-start(bf16[128,1024]{1,0:T(8,128)(2,1)S(1)} %get-tuple-element.31), channel_id=1, source_target_pairs={{0,6},{2,0},{4,2},{6,4},{1,7},{3,1},{5,3},{7,5},{8,14},{10,8},{12,... | collective-permute-start | bytes 786440 | tf_op jit(solution)/shard_map/ppermute | solution.py:13
  260.6 15.1 %collective-permute-start.8 = (bf16[128,1024]{1,0:T(8,128)(2,1)S(1)}, bf16[128,1024]{1,0:T(8,128)(2,1)S(1)}, u32[]{:S(2)}, u32[]{:S(2)}) collective-permute-start(bf16[128,1024]{1,0:T(8,128)(2,1)S(1)} %get-tuple-element.26), channel_id=1, source_target_pairs={{0,2},{2,4},{4,6},{6,0},{1,3},{3,5},{5,7},{7,1},{8,10},{10,12},{12... | collective-permute-start | bytes 786440 | tf_op jit(solution)/shard_map/ppermute | solution.py:13
  261.5 20.2 %collective-permute-start.10 = (bf16[128,1024]{1,0:T(8,128)(2,1)S(1)}, bf16[128,1024]{1,0:T(8,128)(2,1)S(1)}, u32[]{:S(2)}, u32[]{:S(2)}) collective-permute-start(bf16[128,1024]{1,0:T(8,128)(2,1)S(1)} %get-tuple-element.27), channel_id=1, source_target_pairs={{0,4},{2,6},{4,0},{6,2},{1,5},{3,7},{5,1},{7,3},{8,12},{10,14},{12... | collective-permute-start | bytes 786440 | tf_op jit(solution)/shard_map/ppermute | solution.py:13
  265.5 16.3 %collective-permute-start.9 = (bf16[128,1024]{1,0:T(8,128)(2,1)S(1)}, bf16[128,1024]{1,0:T(8,128)(2,1)S(1)}, u32[]{:S(2)}, u32[]{:S(2)}) collective-permute-start(bf16[128,1024]{1,0:T(8,128)(2,1)S(1)} %get-tuple-element.28), channel_id=1, source_target_pairs={{0,6},{2,0},{4,2},{6,4},{1,7},{3,1},{5,3},{7,5},{8,14},{10,8},{12,... | collective-permute-start | bytes 786440 | tf_op jit(solution)/shard_map/ppermute | solution.py:13
  271.9 12.5 %collective-permute-start.38 = (bf16[128,512]{1,0:T(8,128)(2,1)S(1)}, bf16[128,512]{1,0:T(8,128)(2,1)S(1)}, u32[]{:S(2)}, u32[]{:S(2)}) collective-permute-start(bf16[128,512]{1,0:T(8,128)(2,1)S(1)} %slice.210), channel_id=1, source_target_pairs={{0,8},{8,0},{1,9},{9,1},{2,10},{10,2},{3,11},{11,3},{4,12},{12,4},... | collective-permute-start | bytes 393224 | tf_op jit(solution)/shard_map/ppermute | solution.py:13
  (40 other events, 312.6 us)
Sparse Core Ops, SparseCore 0:
  79.2 51.9 reduce-scatter.1
  195.2 43.7 all-gather.1

commit v2 on v1

v2 whole, which is shorter than its diff:
```python
import jax
import jax.numpy as jnp
from jax import lax
from jax.experimental import pallas as pl
from jax.experimental.layout import Layout, with_layout_constraint
from jax.sharding import Mesh
from jax.sharding import PartitionSpec as P

F32 = jnp.float32
BF16 = jnp.bfloat16


def shift(v, axis, by):
    n = lax.axis_size(axis)
    return lax.ppermute(v, axis, [(i, (i + by) % n) for i in range(n)])


def join(*values):
    return lax.optimization_barrier(values)


def part(v, index, size, dim):
    return lax.dynamic_slice_in_dim(v, index * size, size, dim)


def put(base, piece, row, col=0):
    return lax.dynamic_update_slice(base, piece, (jnp.int32(row), jnp.int32(col)))


def dot(left, right):
    return jnp.dot(left, right, preferred_element_type=F32)


def dot_t(left, right):
    return lax.dot_general(left, right, (((1,), (1,)), ((), ())), preferred_element_type=F32)


def product_kernel(left_ref, right_ref, out_ref):
    out_ref[...] = dot_t(left_ref[...], right_ref[...]).astype(out_ref.dtype)


def slope_product(left, right):
    m, k = left.shape
    n = right.shape[0]
    tile = m // 4
    return pl.pallas_call(
        product_kernel,
        grid=(4,),
        in_specs=[
            pl.BlockSpec((tile, k), lambda i: (i, 0)),
            pl.BlockSpec((n, k), lambda i: (0, 0)),
        ],
        out_specs=pl.BlockSpec((tile, n), lambda i: (i, 0)),
        out_shape=jax.ShapeDtypeStruct((m, n), BF16),
        cost_estimate=pl.CostEstimate(flops=int(4e10), transcendentals=0, bytes_accessed=0),
    )(left, right)


def add(left, right):
    return (left.astype(F32) + right.astype(F32)).astype(BF16)


def both_ways(up, down):
    up, down = join(up, down)
    return shift(up, "z", 1), shift(down, "z", -1)


def reduce_cores(product, away, stay):
    return product(stay) + shift(product(away).astype(BF16), "c", 1).astype(F32)


def reduce_chips(v):
    rows = v.shape[0] // 4
    sends = join(*(v[j * rows:(j + 1) * rows].astype(BF16) for j in (2, 1, 3)))
    total = v[:rows]
    for piece, by in zip(sends, (2, 1, -1)):
        total = total + shift(piece, "x", by).astype(F32)
    return total


def local(fwd_in, grad_in, saved_gate, saved_up, gate_weight, up_weight, down_weight):
    inputs = fwd_in[0]
    grads = grad_in[0]
    w_gate, w_up, w_down = gate_weight[0], up_weight[0], down_weight[0]
    z, y = lax.axis_index("z"), lax.axis_index("y")
    x, c = lax.axis_index("x"), lax.axis_index("c")
    rows, feats = inputs.shape
    cols = w_gate.shape[1] // 2
    cut = 4 * cols // 7

    def owner(k):
        return (z + k + 8) % 8

    def place(k):
        return 4 * ((owner(k) + c) % 2) + (owner(k) // 2 + 4 - x) % 4

    tokens = jnp.stack([inputs, grads])
    w_away = jnp.concatenate([part(w_gate, 1 - y, cols, 1), part(w_up, 1 - y, cols, 1)], axis=1)
    tokens_got = shift(tokens, "y", 1)
    tokens_got, w_away = join(tokens_got, w_away)
    tokens = jnp.concatenate([inputs, tokens_got[0], grads, tokens_got[1]], axis=1)
    (tokens,) = join(lax.all_gather(tokens, ("x", "c"), axis=0, tiled=True))
    w_got = shift(w_away, "y", 1)
    down_away = part(w_down, 1 - y, cols, 0)
    w_both = jnp.zeros((2 * feats, 2 * cols), BF16)
    w_both = put(w_both, part(w_gate, y, cols, 1), 0)
    w_both = put(w_both, part(w_up, y, cols, 1), 0, cols)
    down_kept = part(w_down, y, cols, 0)
    saved = jnp.concatenate([saved_gate[0], saved_up[0]], axis=0)
    saved_away, saved = part(saved, 1 - y, cols, 1), part(saved, y, cols, 1)
    w_got, w_both, down_away, down_kept, saved, saved_away = join(
        w_got, w_both, down_away, down_kept, saved, saved_away
    )

    down_got = shift(down_away, "y", 1)
    (w_both,) = join(put(w_both, w_got, feats))
    both = dot(tokens[:, :2 * feats], w_both)
    both = both.astype(BF16)
    ready = both
    both = lax.psum_scatter(both, "z", scatter_dimension=0, tiled=True)
    saved_got = shift(saved_away, "y", 1)
    half = rows // 2
    saved = jnp.where(
        y == 0,
        jnp.concatenate([saved[:half], saved_got[:half], saved[half:], saved_got[half:]]),
        jnp.concatenate([saved_got[:half], saved[:half], saved_got[half:], saved[half:]]),
    )
    down_got, saved, ready = join(down_got, saved, ready)
    (down_pair,) = join(jnp.concatenate([down_kept, down_got], axis=1))
    term = slope_product(tokens[:, 2 * feats:], down_pair)

    def block(k):
        return part(term, owner(k), rows, 0)

    a = block(4)
    up, down = join(*both_ways(a[:, :cut], a[:, cut:]))
    a, b = block(3), block(-3)
    up = jnp.concatenate([add(a[:, :cut], up), a[:, cut:]], axis=1)
    down = jnp.concatenate([b[:, :cut], add(b[:, cut:], down)], axis=1)
    up, down = join(*both_ways(up, down))
    up, down = join(*both_ways(add(block(2), up), add(block(-2), down)))
    up, down = join(*both_ways(add(block(1), up), add(block(-1), down)))
    slope = block(0).astype(F32) + up.astype(F32) + down.astype(F32)
    gvals, uvals = saved[:rows].astype(F32), saved[rows:].astype(F32)
    sig = jax.nn.sigmoid(gvals)
    gate_grad = (slope * uvals * sig * (1.0 + gvals * (1.0 - sig))).astype(BF16)
    up_grad = (slope * gvals * sig).astype(BF16)
    pieces, both = join(jnp.concatenate([gate_grad, up_grad], axis=1), both)
    pieces = lax.all_gather(pieces, "z", axis=0, tiled=True)
    pieces = with_layout_constraint(pieces, Layout(major_to_minor=(0, 1)))

    both = both.astype(F32)
    hidden = (jax.nn.silu(both[:, :cols]) * both[:, cols:]).astype(BF16)
    spots = put(jnp.zeros((8 * rows, cols), BF16), hidden, place(0) * rows)
    up, down = hidden, hidden
    for k in (1, 2, 3):
        up, down = join(*both_ways(up, down))
        spots = put(put(spots, up, place(-k) * rows), down, place(k) * rows)
    up, down = both_ways(up[:, :cut], down[:, cut:])
    spots = put(put(spots, up, place(4) * rows), down, place(4) * rows, cut)
    mixed = reduce_cores(lambda v: dot(v, down_pair), spots[4 * rows:], spots[:4 * rows])
    pieces, mixed = join(pieces, mixed)

    def chosen(core):
        return jnp.concatenate(
            [part(pieces, 2 * ((x + j) % 4) + core, rows, 0) for j in range(4)], axis=0
        )

    mixed = reduce_chips(mixed)
    back = reduce_cores(lambda v: dot_t(v, w_both), *join(chosen(1 - c), chosen(c)))
    back = reduce_chips(back)
    (ends,) = join(jnp.stack([mixed[:, feats:], back[:, feats:]]).astype(BF16))
    ends = shift(ends, "y", 1).astype(F32)
    forward_result = (inputs.astype(F32) + mixed[:, :feats] + ends[0]).astype(BF16)
    backward_result = (grads.astype(F32) + back[:, :feats] + ends[1]).astype(BF16)

    outgoing = jnp.where(lax.axis_index("s") == 0, forward_result, backward_result)
    received = shift(outgoing, "s", 1)
    return (forward_result[None], backward_result[None], received[None])


def solution(mesh):
    fine = Mesh(mesh.devices.reshape(2, 8, 2, 4, 2), ("s", "z", "y", "x", "c"))
    tokens = P("s", ("x", "c"), ("z", "y"))
    hidden = P("s", ("z", "y"), ("x", "c"))
    return jax.shard_map(
        local,
        mesh=fine,
        in_specs=(tokens, tokens, hidden, hidden, hidden, hidden, tokens),
        out_specs=(tokens, tokens, tokens),
        check_vma=False,
    )
```

time: 307 us -> 268 us (0.87); the launches traced: 302 us -> 267 us
  local copies, waits for them, and re-layouts: 34.5 us -> 17.8 us
  matrix products: 32.1 us -> 22.1 us
  starting transfers between devices: 58.3 us -> 50.6 us
  Pallas kernels: 0 us -> 5.99 us
  waiting for transfers between devices: 148 us -> 143 us
    unnamed x53 -> x23, local copies, waits for them, and re-layouts: 13.9 us -> 1.71 us
    dot_general x4 -> x5, matrix products: 32.1 us -> 22.1 us  [the longest x3 13.9 us: dot(): return jnp.dot(left, right, preferred_element_type=F32)]
    ppermute x40 -> x30, waiting for transfers between devices: 148 us -> 140 us  [shift(): return lax.ppermute(v, axis, [(i, (i + by) % n) for i in range(n)])]
    ppermute x40 -> x30, starting transfers between devices: 58.2 us -> 50.5 us  [shift(): return lax.ppermute(v, axis, [(i, (i + by) % n) for i in range(n)])]
    pallas_call x0 -> x1, Pallas kernels: none -> 5.99 us  [slope_product(): pl.pallas_call(product_kernel, grid=(4,), in_specs=[pl.BlockSpec((tile, k...]
    slice x9, local copies, waits for them, and re-layouts: 0.66 us -> 5.33 us  [the longest x1 3.07 us: local(): term = slope_product(tokens[:, 2 * feats:], down_pair)]
    concatenate x2 -> x0, local copies, waits for them, and re-layouts: 3.58 us -> none  [gather_tensor(): return jnp.concatenate([chips, shift(chips, 'c', 1)], axis=0)]
    all_gather x1 -> x2, waiting for transfers between devices: 0.02 us -> 3.39 us  [the longest x1 3.39 us: local(): pieces = lax.all_gather(pieces, 'z', axis=0, tiled=True)]
  transfers between devices with their start and end apart: 42 -> 33, of which waited for: 30 -> 25; matrix products, arithmetic and copies ran while one was open for 19% -> 15% of each run, Pallas kernels for 0% -> 2%
where the time goes in v2:
time: 268 us; the launch traced here: 267 us
  waiting for transfers between devices  143 us (53%)
  starting transfers between devices  50.6 us (19%)
  matrix products  22.1 us (8%)
  local copies, waits for them, and re-layouts  17.8 us (7%)
  between operations  14.2 us (5%)
  other arithmetic  12.9 us (5%)
  Pallas kernels  5.99 us (2%)
    ppermute x30, waiting for transfers between devices, shift(): return lax.ppermute(v, axis, [(i, (i + by) % n) for i in range(n)])  140 us
    ppermute x30, starting transfers between devices, shift(): return lax.ppermute(v, axis, [(i, (i + by) % n) for i in range(n)])  50.5 us
    dot_general x3, matrix products, dot(): return jnp.dot(left, right, preferred_element_type=F32)  13.9 us
    dot_general x2, matrix products, dot_t(): lax.dot_general(left, right, (((1,), (1,)), ((), ())), preferred_element_...  8.25 us
    pallas_call x1, Pallas kernels, slope_product(): pl.pallas_call(product_kernel, grid=(4,), in_specs=[pl.BlockSpec((tile, k...  5.99 us
  transfers between devices with their start and end apart: 33, of which 25 were waited for; matrix products, arithmetic and copies ran while one was open for 15% of the time, Pallas kernels for 2%

profile of v2, /device:TPU:8, one launch (start us, length us, event | category | flops | bytes accessed | tf_op | source)
XLA Modules:
  0.0 267.1 jit_solution(5426395410110944724)
XLA Ops:
  13.0 5.9 %collective-permute-done = bf16[2,128,512]{2,1,0:T(8,128)(2,1)} collective-permute-done((bf16[2,128,512]{2,1,0:T(8,128)(2,1)}, bf16[2,128,512]{2,1,0:T(8,128)(2,1)}, u32[]{:S(2)}, u32[]{:S(2)}) %collective-permute-start) | collective-permute-done | bytes 262176 | tf_op jit(solution)/shard_map/ppermute | solution.py:15
  28.5 34.9 %collective-permute-done.1 = bf16[512,1792]{1,0:T(8,128)(2,1)S(1)} collective-permute-done((bf16[512,1792]{1,0:T(8,128)(2,1)S(1)}, bf16[512,1792]{1,0:T(8,128)(2,1)S(1)}, u32[]{:S(2)}, u32[]{:S(2)}) %collective-permute-start.1) | collective-permute-done | bytes 1835040 | tf_op jit(solution)/shard_map/ppermute | solution.py:15
  67.0 8.5 %convolution_convert_fusion = bf16[1024,1792]{1,0:T(8,128)(2,1)} fusion(bf16[1024,1792]{1,0:T(8,128)(2,1)} %constant_dynamic-update-slice_fusion.8, bf16[1024,2048]{1,0:T(8,128)(2,1)} %all-gather.3.cloned.1.call-done), kind=kOutput, calls=%fused_computation | convolution fusion | flops 3759931392 | bytes 9437184 | tf_op jit(solution)/shard_map/dot_general | solution.py:31
  77.7 13.9 %collective-permute-done.3 = bf16[128,896]{1,0:T(8,128)(2,1)S(1)} collective-permute-done((bf16[128,896]{1,0:T(8,128)(2,1)S(1)}, bf16[128,896]{1,0:T(8,128)(2,1)S(1)}, u32[]{:S(2)}, u32[]{:S(2)}) %collective-permute-start.3) | collective-permute-done | bytes 229408 | tf_op jit(solution)/shard_map/ppermute | solution.py:15
  91.7 3.1 %slice.156.left_ref = bf16[1024,1024]{1,0:T(8,128)(2,1)} slice(bf16[1024,2048]{1,0:T(8,128)(2,1)} %all-gather.3.cloned.1.call-done), slice={[0:1024], [1024:2048]} | slice | bytes 4194304 | tf_op jit(solution)/shard_map/slice | solution.py:130
  96.4 6.0 %shard_map.94 = bf16[1024,896]{1,0:T(8,128)(2,1)} custom-call(bf16[1024,1024]{1,0:T(8,128)(2,1)} %slice.156.left_ref, bf16[896,1024]{1,0:T(8,128)(2,1)} %pad_maximum_fusion.1.right_ref), custom_call_target="tpu_custom_call" | custom-call | flops 40000000000 | tf_op jit(solution)/shard_map/pallas_call | solution.py:46
  106.5 4.0 %collective-permute-start.5 = (bf16[128,384]{1,0:T(8,128)(2,1)S(1)}, bf16[128,384]{1,0:T(8,128)(2,1)S(1)}, u32[]{:S(2)}, u32[]{:S(2)}) collective-permute-start(bf16[128,384]{1,0:T(8,128)(2,1)S(1)} %get-tuple-element.65), channel_id=1, source_target_pairs={{0,112},{16,0},{32,16},{48,32},{64,48},{80,64},{96,80},{112,96},{1... | collective-permute-start | bytes 294920 | tf_op jit(solution)/shard_map/ppermute | solution.py:15
  110.5 4.4 %collective-permute-done.5 = bf16[128,384]{1,0:T(8,128)(2,1)S(1)} collective-permute-done((bf16[128,384]{1,0:T(8,128)(2,1)S(1)}, bf16[128,384]{1,0:T(8,128)(2,1)S(1)}, u32[]{:S(2)}, u32[]{:S(2)}) %collective-permute-start.5) | collective-permute-done | bytes 98336 | tf_op jit(solution)/shard_map/ppermute | solution.py:15
  119.2 3.2 %collective-permute-start.7 = (bf16[128,896]{1,0:T(8,128)(2,1)S(1)}, bf16[128,896]{1,0:T(8,128)(2,1)S(1)}, u32[]{:S(2)}, u32[]{:S(2)}) collective-permute-start(bf16[128,896]{1,0:T(8,128)(2,1)S(1)} %get-tuple-element.69), channel_id=1, source_target_pairs={{0,112},{16,0},{32,16},{48,32},{64,48},{80,64},{96,80},{112,96},{1... | collective-permute-start | bytes 688136 | tf_op jit(solution)/shard_map/ppermute | solution.py:15
  122.4 10.3 %collective-permute-done.6 = bf16[128,896]{1,0:T(8,128)(2,1)S(1)} collective-permute-done((bf16[128,896]{1,0:T(8,128)(2,1)}, bf16[128,896]{1,0:T(8,128)(2,1)S(1)}, u32[]{:S(2)}, u32[]{:S(2)}) %collective-permute-start.6) | collective-permute-done | bytes 229408 | tf_op jit(solution)/shard_map/ppermute | solution.py:15
  136.2 4.0 %collective-permute-done.8 = bf16[128,896]{1,0:T(8,128)(2,1)S(1)} collective-permute-done((bf16[128,896]{1,0:T(8,128)(2,1)S(1)}, bf16[128,896]{1,0:T(8,128)(2,1)S(1)}, u32[]{:S(2)}, u32[]{:S(2)}) %collective-permute-start.8) | collective-permute-done | bytes 229408 | tf_op jit(solution)/shard_map/ppermute | solution.py:15
  143.8 3.9 %collective-permute-done.10 = bf16[128,896]{1,0:T(8,128)(2,1)S(1)} collective-permute-done((bf16[128,896]{1,0:T(8,128)(2,1)S(1)}, bf16[128,896]{1,0:T(8,128)(2,1)S(1)}, u32[]{:S(2)}, u32[]{:S(2)}) %collective-permute-start.10) | collective-permute-done | bytes 229408 | tf_op jit(solution)/shard_map/ppermute | solution.py:15
  156.5 5.0 %collective-permute-done.12 = bf16[128,896]{1,0:T(8,128)(2,1)S(1)} collective-permute-done((bf16[128,896]{1,0:T(8,128)(2,1)S(1)}, bf16[128,896]{1,0:T(8,128)(2,1)S(1)}, u32[]{:S(2)}, u32[]{:S(2)}) %collective-permute-start.12) | collective-permute-done | bytes 229408 | tf_op jit(solution)/shard_map/ppermute | solution.py:15
  165.6 8.9 %collective-permute-done.14 = bf16[128,896]{1,0:T(8,128)(2,1)S(1)} collective-permute-done((bf16[128,896]{1,0:T(8,128)(2,1)S(1)}, bf16[128,896]{1,0:T(8,128)(2,1)S(1)}, u32[]{:S(2)}, u32[]{:S(2)}) %collective-permute-start.14) | collective-permute-done | bytes 229408 | tf_op jit(solution)/shard_map/ppermute | solution.py:15
  179.8 9.1 %collective-permute-done.16 = bf16[128,896]{1,0:T(8,128)(2,1)S(1)} collective-permute-done((bf16[128,896]{1,0:T(8,128)(2,1)S(1)}, bf16[128,896]{1,0:T(8,128)(2,1)S(1)}, u32[]{:S(2)}, u32[]{:S(2)}) %collective-permute-start.16) | collective-permute-done | bytes 229408 | tf_op jit(solution)/shard_map/ppermute | solution.py:15
  192.5 5.7 %collective-permute-done.18 = bf16[128,512]{1,0:T(8,128)(2,1)S(1)} collective-permute-done((bf16[128,512]{1,0:T(8,128)(2,1)S(1)}, bf16[128,512]{1,0:T(8,128)(2,1)S(1)}, u32[]{:S(2)}, u32[]{:S(2)}) %collective-permute-start.18) | collective-permute-done | bytes 131104 | tf_op jit(solution)/shard_map/ppermute | solution.py:15
  206.5 3.4 %all-gather.5.cloned.1.call-done = bf16[1024,1792]{1,0:T(8,128)(2,1)} async-done(((bf16[128,1792]{1,0:T(8,128)(2,1)}), bf16[1024,1792]{1,0:T(8,128)(2,1)}) %all-gather.5.cloned.1.call-update) | async-done | bytes 3670032 | tf_op jit(solution)/shard_map/all_gather | solution.py:149
  212.4 4.1 %convolution_convert_fusion.2 = bf16[512,1024]{1,0:T(8,128)(2,1)S(1)} fusion(bf16[512,1792]{1,0:T(8,128)(2,1)S(1)} %pad_maximum_fusion.2, bf16[1024,1792]{1,0:T(8,128)(2,1)} %constant_dynamic-update-slice_fusion.8), kind=kOutput, calls=%fused_computation.9 | convolution fusion | flops 1879572480 | bytes 6553600 | tf_op jit(solution)/shard_map/dot_general | solution.py:35
  216.9 3.1 %collective-permute-start.21 = (bf16[128,1024]{1,0:T(8,128)(2,1)S(1)}, bf16[128,1024]{1,0:T(8,128)(2,1)S(1)}, u32[]{:S(2)}, u32[]{:S(2)}) collective-permute-start(bf16[128,1024]{1,0:T(8,128)(2,1)S(1)} %get-tuple-element.98), channel_id=1, source_target_pairs={{0,4},{2,6},{4,0},{6,2},{1,5},{3,7},{5,1},{7,3},{8,12},{10,14},{12... | collective-permute-start | bytes 786440 | tf_op jit(solution)/shard_map/ppermute | solution.py:15
  223.3 4.1 %fusion.24 = (bf16[512,1024]{1,0:T(8,128)(2,1)S(1)}, f32[512,1024]{1,0:T(8,128)S(1)}) fusion(bf16[512,1024]{1,0:T(8,128)(2,1)S(1)} %collective-permute-done.24, bf16[512,1792]{1,0:T(8,128)(2,1)S(1)} %pad_maximum_fusion.3, bf16[1024,1792]{1,0:T(8,128)(2,1)} %constant_dynamic-update-slice_fusion.8), kind=kOutput, calls=%fused_computation.90 | convolution fusion | flops 1880621056 | bytes 9699328 | tf_op jit(solution)/shard_map/dot_general | solution.py:35
  233.6 5.3 %collective-permute-done.25 = bf16[128,1024]{1,0:T(8,128)(2,1)S(1)} collective-permute-done((bf16[128,1024]{1,0:T(8,128)(2,1)S(1)}, bf16[128,1024]{1,0:T(8,128)(2,1)S(1)}, u32[]{:S(2)}, u32[]{:S(2)}) %collective-permute-start.25) | collective-permute-done | bytes 262176 | tf_op jit(solution)/shard_map/ppermute | solution.py:15
  238.9 5.1 %collective-permute-done.26 = bf16[128,1024]{1,0:T(8,128)(2,1)S(1)} collective-permute-done((bf16[128,1024]{1,0:T(8,128)(2,1)S(1)}, bf16[128,1024]{1,0:T(8,128)(2,1)S(1)}, u32[]{:S(2)}, u32[]{:S(2)}) %collective-permute-start.26) | collective-permute-done | bytes 262176 | tf_op jit(solution)/shard_map/ppermute | solution.py:15
  247.1 7.0 %collective-permute-done.28 = bf16[2,128,512]{2,1,0:T(8,128)(2,1)S(1)} collective-permute-done((bf16[2,128,512]{2,1,0:T(8,128)(2,1)S(1)}, bf16[2,128,512]{2,1,0:T(8,128)(2,1)S(1)}, u32[]{:S(2)}, u32[]{:S(2)}) %collective-permute-start.28) | collective-permute-done | bytes 262176 | tf_op jit(solution)/shard_map/ppermute | solution.py:15
  255.7 4.2 %collective-permute-done.29 = bf16[128,512]{1,0:T(8,128)(2,1)S(1)} collective-permute-done((bf16[128,512]{1,0:T(8,128)(2,1)S(1)}, bf16[128,512]{1,0:T(8,128)(2,1)S(1)}, u32[]{:S(2)}, u32[]{:S(2)}) %collective-permute-start.29) | collective-permute-done | bytes 131104 | tf_op jit(solution)/shard_map/ppermute | solution.py:15
  (125 shorter events, 85.7 us)
Async XLA Ops:
  7.2 59.8 %all-gather.3.cloned.1.call-start = ((), (), s32[]{:S(2)}) async-start(), calls=%async_computation.1 | async-start | bytes 4718592 | tf_op jit(solution)/shard_map/all_gather | solution.py:102
  9.1 9.9 %collective-permute-start = (bf16[2,128,512]{2,1,0:T(8,128)(2,1)}, bf16[2,128,512]{2,1,0:T(8,128)(2,1)}, u32[]{:S(2)}, u32[]{:S(2)}) collective-permute-start(bf16[2,128,512]{2,1,0:T(8,128)(2,1)} %pad_maximum_fusion.6), channel_id=1, source_target_pairs={{0,8},{8,0},{1,9},{9,1},{2,10},{10,2},{3,11},{11,3},{4,12},{12,4},... | collective-permute-start | bytes 786440 | tf_op jit(solution)/shard_map/ppermute | solution.py:15
  20.8 130.9 %reduce-scatter.2.cloned.1.call-start = ((), (), s32[]{:S(2)}) async-start(), calls=%async_computation.2 | async-start | bytes 4128768 | tf_op jit(solution)/shard_map/reduce_scatter | solution.py:120
  20.9 42.5 %collective-permute-start.1 = (bf16[512,1792]{1,0:T(8,128)(2,1)S(1)}, bf16[512,1792]{1,0:T(8,128)(2,1)S(1)}, u32[]{:S(2)}, u32[]{:S(2)}) collective-permute-start(bf16[512,1792]{1,0:T(8,128)(2,1)S(1)} %pad_maximum_fusion), channel_id=1, source_target_pairs={{0,8},{8,0},{1,9},{9,1},{2,10},{10,2},{3,11},{11,3},{4,12},{12,4},... | collective-permute-start | bytes 5505032 | tf_op jit(solution)/shard_map/ppermute | solution.py:15
  64.7 30.1 %collective-permute-start.2 = (bf16[896,512]{1,0:T(8,128)(2,1)}, bf16[896,512]{1,0:T(8,128)(2,1)S(1)}, u32[]{:S(2)}, u32[]{:S(2)}) collective-permute-start(bf16[896,512]{1,0:T(8,128)(2,1)} %get-tuple-element.58), channel_id=1, source_target_pairs={{0,8},{8,0},{1,9},{9,1},{2,10},{10,2},{3,11},{11,3},{4,12},{12,4},... | collective-permute-start | bytes 2752520 | tf_op jit(solution)/shard_map/ppermute | solution.py:15
  75.5 134.4 %all-gather.5.cloned.1.call-start = ((), (), s32[]{:S(2)}) async-start(), calls=%async_computation.3 | async-start | bytes 4128768 | tf_op jit(solution)/shard_map/all_gather | solution.py:149
  76.4 15.2 %collective-permute-start.3 = (bf16[128,896]{1,0:T(8,128)(2,1)S(1)}, bf16[128,896]{1,0:T(8,128)(2,1)S(1)}, u32[]{:S(2)}, u32[]{:S(2)}) collective-permute-start(bf16[128,896]{1,0:T(8,128)(2,1)S(1)} %copy-done.10), channel_id=1, source_target_pairs={{0,8},{8,0},{1,9},{9,1},{2,10},{10,2},{3,11},{11,3},{4,12},{12,4},... | collective-permute-start | bytes 688136 | tf_op jit(solution)/shard_map/ppermute | solution.py:15
  104.5 12.1 %collective-permute-start.4 = (bf16[128,512]{1,0:T(8,128)(2,1)S(1)}, bf16[128,512]{1,0:T(8,128)(2,1)S(1)}, u32[]{:S(2)}, u32[]{:S(2)}) collective-permute-start(bf16[128,512]{1,0:T(8,128)(2,1)S(1)} %get-tuple-element.64), channel_id=1, source_target_pairs={{0,16},{16,32},{32,48},{48,64},{64,80},{80,96},{96,112},{112,0},{1... | collective-permute-start | bytes 393224 | tf_op jit(solution)/shard_map/ppermute | solution.py:15
  106.5 8.4 %collective-permute-start.5 = (bf16[128,384]{1,0:T(8,128)(2,1)S(1)}, bf16[128,384]{1,0:T(8,128)(2,1)S(1)}, u32[]{:S(2)}, u32[]{:S(2)}) collective-permute-start(bf16[128,384]{1,0:T(8,128)(2,1)S(1)} %get-tuple-element.65), channel_id=1, source_target_pairs={{0,112},{16,0},{32,16},{48,32},{64,48},{80,64},{96,80},{112,96},{1... | collective-permute-start | bytes 294920 | tf_op jit(solution)/shard_map/ppermute | solution.py:15
  119.2 13.6 %collective-permute-start.6 = (bf16[128,896]{1,0:T(8,128)(2,1)}, bf16[128,896]{1,0:T(8,128)(2,1)S(1)}, u32[]{:S(2)}, u32[]{:S(2)}) collective-permute-start(bf16[128,896]{1,0:T(8,128)(2,1)} %get-tuple-element.68), channel_id=1, source_target_pairs={{0,16},{16,32},{32,48},{48,64},{64,80},{80,96},{96,112},{112,0},{1... | collective-permute-start | bytes 688136 | tf_op jit(solution)/shard_map/ppermute | solution.py:15
  119.2 13.6 %collective-permute-start.7 = (bf16[128,896]{1,0:T(8,128)(2,1)S(1)}, bf16[128,896]{1,0:T(8,128)(2,1)S(1)}, u32[]{:S(2)}, u32[]{:S(2)}) collective-permute-start(bf16[128,896]{1,0:T(8,128)(2,1)S(1)} %get-tuple-element.69), channel_id=1, source_target_pairs={{0,112},{16,0},{32,16},{48,32},{64,48},{80,64},{96,80},{112,96},{1... | collective-permute-start | bytes 688136 | tf_op jit(solution)/shard_map/ppermute | solution.py:15
  153.2 8.3 %collective-permute-start.12 = (bf16[128,896]{1,0:T(8,128)(2,1)S(1)}, bf16[128,896]{1,0:T(8,128)(2,1)S(1)}, u32[]{:S(2)}, u32[]{:S(2)}) collective-permute-start(bf16[128,896]{1,0:T(8,128)(2,1)S(1)} %get-tuple-element.84), channel_id=1, source_target_pairs={{0,16},{16,32},{32,48},{48,64},{64,80},{80,96},{96,112},{112,0},{1... | collective-permute-start | bytes 688136 | tf_op jit(solution)/shard_map/ppermute | solution.py:15
  162.3 12.2 %collective-permute-start.14 = (bf16[128,896]{1,0:T(8,128)(2,1)S(1)}, bf16[128,896]{1,0:T(8,128)(2,1)S(1)}, u32[]{:S(2)}, u32[]{:S(2)}) collective-permute-start(bf16[128,896]{1,0:T(8,128)(2,1)S(1)} %collective-permute-done.12), channel_id=1, source_target_pairs={{0,16},{16,32},{32,48},{48,64},{64,80},{80,96},{96,112},{112,0},{1... | collective-permute-start | bytes 688136 | tf_op jit(solution)/shard_map/ppermute | solution.py:15
  164.1 12.5 %collective-permute-start.15 = (bf16[128,896]{1,0:T(8,128)(2,1)S(1)}, bf16[128,896]{1,0:T(8,128)(2,1)S(1)}, u32[]{:S(2)}, u32[]{:S(2)}) collective-permute-start(bf16[128,896]{1,0:T(8,128)(2,1)S(1)} %collective-permute-done.13), channel_id=1, source_target_pairs={{0,112},{16,0},{32,16},{48,32},{64,48},{80,64},{96,80},{112,96},{1... | collective-permute-start | bytes 688136 | tf_op jit(solution)/shard_map/ppermute | solution.py:15
  176.5 12.4 %collective-permute-start.16 = (bf16[128,896]{1,0:T(8,128)(2,1)S(1)}, bf16[128,896]{1,0:T(8,128)(2,1)S(1)}, u32[]{:S(2)}, u32[]{:S(2)}) collective-permute-start(bf16[128,896]{1,0:T(8,128)(2,1)S(1)} %collective-permute-done.14), channel_id=1, source_target_pairs={{0,16},{16,32},{32,48},{48,64},{64,80},{80,96},{96,112},{112,0},{1... | collective-permute-start | bytes 688136 | tf_op jit(solution)/shard_map/ppermute | solution.py:15
  178.2 10.9 %collective-permute-start.17 = (bf16[128,896]{1,0:T(8,128)(2,1)S(1)}, bf16[128,896]{1,0:T(8,128)(2,1)S(1)}, u32[]{:S(2)}, u32[]{:S(2)}) collective-permute-start(bf16[128,896]{1,0:T(8,128)(2,1)S(1)} %collective-permute-done.15), channel_id=1, source_target_pairs={{0,112},{16,0},{32,16},{48,32},{64,48},{80,64},{96,80},{112,96},{1... | collective-permute-start | bytes 688136 | tf_op jit(solution)/shard_map/ppermute | solution.py:15
  189.1 9.0 %collective-permute-start.18 = (bf16[128,512]{1,0:T(8,128)(2,1)S(1)}, bf16[128,512]{1,0:T(8,128)(2,1)S(1)}, u32[]{:S(2)}, u32[]{:S(2)}) collective-permute-start(bf16[128,512]{1,0:T(8,128)(2,1)S(1)} %slice.138), channel_id=1, source_target_pairs={{0,16},{16,32},{32,48},{48,64},{64,80},{80,96},{96,112},{112,0},{1... | collective-permute-start | bytes 393224 | tf_op jit(solution)/shard_map/ppermute | solution.py:15
  216.9 11.5 %collective-permute-start.21 = (bf16[128,1024]{1,0:T(8,128)(2,1)S(1)}, bf16[128,1024]{1,0:T(8,128)(2,1)S(1)}, u32[]{:S(2)}, u32[]{:S(2)}) collective-permute-start(bf16[128,1024]{1,0:T(8,128)(2,1)S(1)} %get-tuple-element.98), channel_id=1, source_target_pairs={{0,4},{2,6},{4,0},{6,2},{1,5},{3,7},{5,1},{7,3},{8,12},{10,14},{12... | collective-permute-start | bytes 786440 | tf_op jit(solution)/shard_map/ppermute | solution.py:15
  220.0 13.3 %collective-permute-start.22 = (bf16[128,1024]{1,0:T(8,128)(2,1)S(1)}, bf16[128,1024]{1,0:T(8,128)(2,1)S(1)}, u32[]{:S(2)}, u32[]{:S(2)}) collective-permute-start(bf16[128,1024]{1,0:T(8,128)(2,1)S(1)} %get-tuple-element.99), channel_id=1, source_target_pairs={{0,2},{2,4},{4,6},{6,0},{1,3},{3,5},{5,7},{7,1},{8,10},{10,12},{12... | collective-permute-start | bytes 786440 | tf_op jit(solution)/shard_map/ppermute | solution.py:15
  220.7 12.7 %collective-permute-start.23 = (bf16[128,1024]{1,0:T(8,128)(2,1)S(1)}, bf16[128,1024]{1,0:T(8,128)(2,1)S(1)}, u32[]{:S(2)}, u32[]{:S(2)}) collective-permute-start(bf16[128,1024]{1,0:T(8,128)(2,1)S(1)} %get-tuple-element.100), channel_id=1, source_target_pairs={{0,6},{2,0},{4,2},{6,4},{1,7},{3,1},{5,3},{7,5},{8,14},{10,8},{12,... | collective-permute-start | bytes 786440 | tf_op jit(solution)/shard_map/ppermute | solution.py:15
  227.5 11.5 %collective-permute-start.25 = (bf16[128,1024]{1,0:T(8,128)(2,1)S(1)}, bf16[128,1024]{1,0:T(8,128)(2,1)S(1)}, u32[]{:S(2)}, u32[]{:S(2)}) collective-permute-start(bf16[128,1024]{1,0:T(8,128)(2,1)S(1)} %get-tuple-element.104), channel_id=1, source_target_pairs={{0,4},{2,6},{4,0},{6,2},{1,5},{3,7},{5,1},{7,3},{8,12},{10,14},{12... | collective-permute-start | bytes 786440 | tf_op jit(solution)/shard_map/ppermute | solution.py:15
  227.6 16.4 %collective-permute-start.26 = (bf16[128,1024]{1,0:T(8,128)(2,1)S(1)}, bf16[128,1024]{1,0:T(8,128)(2,1)S(1)}, u32[]{:S(2)}, u32[]{:S(2)}) collective-permute-start(bf16[128,1024]{1,0:T(8,128)(2,1)S(1)} %get-tuple-element.105), channel_id=1, source_target_pairs={{0,2},{2,4},{4,6},{6,0},{1,3},{3,5},{5,7},{7,1},{8,10},{10,12},{12... | collective-permute-start | bytes 786440 | tf_op jit(solution)/shard_map/ppermute | solution.py:15
  228.4 15.9 %collective-permute-start.27 = (bf16[128,1024]{1,0:T(8,128)(2,1)S(1)}, bf16[128,1024]{1,0:T(8,128)(2,1)S(1)}, u32[]{:S(2)}, u32[]{:S(2)}) collective-permute-start(bf16[128,1024]{1,0:T(8,128)(2,1)S(1)} %get-tuple-element.106), channel_id=1, source_target_pairs={{0,6},{2,0},{4,2},{6,4},{1,7},{3,1},{5,3},{7,5},{8,14},{10,8},{12,... | collective-permute-start | bytes 786440 | tf_op jit(solution)/shard_map/ppermute | solution.py:15
  244.5 9.6 %collective-permute-start.28 = (bf16[2,128,512]{2,1,0:T(8,128)(2,1)S(1)}, bf16[2,128,512]{2,1,0:T(8,128)(2,1)S(1)}, u32[]{:S(2)}, u32[]{:S(2)}) collective-permute-start(bf16[2,128,512]{2,1,0:T(8,128)(2,1)S(1)} %pad_maximum_fusion.7), channel_id=1, source_target_pairs={{0,8},{8,0},{1,9},{9,1},{2,10},{10,2},{3,11},{11,3},{4,12},{12,4},... | collective-permute-start | bytes 786440 | tf_op jit(solution)/shard_map/ppermute | solution.py:15
  (20 other events, 151.8 us)
Sparse Core Ops, SparseCore 0:
  20.9 37.5 all-gather.2
  75.6 60.5 reduce-scatter.1
  151.9 57.9 all-gather.4

commit v3 on v2

--- a/solution.py
+++ b/solution.py
@@ -2,6 +2,7 @@
 import jax.numpy as jnp
 from jax import lax
 from jax.experimental import pallas as pl
+from jax.experimental.pallas import tpu as pltpu
 from jax.experimental.layout import Layout, with_layout_constraint
 from jax.sharding import Mesh
 from jax.sharding import PartitionSpec as P
@@ -35,25 +36,34 @@
     return lax.dot_general(left, right, (((1,), (1,)), ((), ())), preferred_element_type=F32)
 
 
-def product_kernel(left_ref, right_ref, out_ref):
-    out_ref[...] = dot_t(left_ref[...], right_ref[...]).astype(out_ref.dtype)
-
-
-def slope_product(left, right):
-    m, k = left.shape
-    n = right.shape[0]
-    tile = m // 4
+def slope_kernel(left_ref, kept_ref, got_ref, out_ref):
+    feats = kept_ref.shape[1]
+    total = dot_t(left_ref[:, :feats], kept_ref[...]) + dot_t(left_ref[:, feats:], got_ref[...])
+    out_ref[...] = total.astype(out_ref.dtype)
+
+
+def gate_kernel(left_ref, kept_ref, got_ref, out_ref):
+    feats = kept_ref.shape[0]
+    total = dot(left_ref[:, :feats], kept_ref[...]) + dot(left_ref[:, feats:], got_ref[...])
+    out_ref[...] = total.astype(out_ref.dtype)
+
+
+def product(kernel, tokens, column, kept, got, width, steps, flops):
+    m, k = tokens.shape[0], tokens.shape[1] // 2
+    half = got.shape
     return pl.pallas_call(
-        product_kernel,
-        grid=(4,),
+        kernel,
+        grid=(steps,),
         in_specs=[
-            pl.BlockSpec((tile, k), lambda i: (i, 0)),
-            pl.BlockSpec((n, k), lambda i: (0, 0)),
+            pl.BlockSpec((m // steps, k), lambda i: (i, column)),
+            pl.BlockSpec(half, lambda i: (0, 0)),
+            pl.BlockSpec(half, lambda i: (0, 0)),
         ],
-        out_specs=pl.BlockSpec((tile, n), lambda i: (i, 0)),
-        out_shape=jax.ShapeDtypeStruct((m, n), BF16),
-        cost_estimate=pl.CostEstimate(flops=int(4e10), transcendentals=0, bytes_accessed=0),
-    )(left, right)
+        out_specs=pl.BlockSpec((m // steps, width), lambda i: (i, 0)),
+        out_shape=jax.ShapeDtypeStruct((m, width), BF16),
+        compiler_params=pltpu.CompilerParams(vmem_limit_bytes=32 << 20),
+        cost_estimate=pl.CostEstimate(flops=flops, transcendentals=0, bytes_accessed=0),
+    )(tokens, kept, got)
 
 
 def add(left, right):
@@ -113,9 +123,7 @@
     )
 
     down_got = shift(down_away, "y", 1)
-    (w_both,) = join(put(w_both, w_got, feats))
-    both = dot(tokens[:, :2 * feats], w_both)
-    both = both.astype(BF16)
+    both = product(gate_kernel, tokens, 0, w_both, w_got, 2 * cols, 4, int(1.5e10))
     ready = both
     both = lax.psum_scatter(both, "z", scatter_dimension=0, tiled=True)
     saved_got = shift(saved_away, "y", 1)
@@ -125,15 +133,17 @@
         jnp.concatenate([saved[:half], saved_got[:half], saved[half:], saved_got[half:]]),
         jnp.concatenate([saved_got[:half], saved[:half], saved_got[half:], saved[half:]]),
     )
-    down_got, saved, ready = join(down_got, saved, ready)
-    (down_pair,) = join(jnp.concatenate([down_kept, down_got], axis=1))
-    term = slope_product(tokens[:, 2 * feats:], down_pair)
+    down_got, saved, ready, w_got = join(down_got, saved, ready, w_got)
+    term = product(slope_kernel, tokens, 1, down_kept, down_got, cols, 2, int(4e10))
 
     def block(k):
         return part(term, owner(k), rows, 0)
 
     a = block(4)
-    up, down = join(*both_ways(a[:, :cut], a[:, cut:]))
+    up, down = both_ways(a[:, :cut], a[:, cut:])
+    down_pair = jnp.concatenate([down_kept, down_got], axis=1)
+    w_both = put(w_both, w_got, feats)
+    up, down, down_pair, w_both = join(up, down, down_pair, w_both)
     a, b = block(3), block(-3)
     up = jnp.concatenate([add(a[:, :cut], up), a[:, cut:]], axis=1)
     down = jnp.concatenate([b[:, :cut], add(b[:, cut:], down)], axis=1)

time: 268 us -> 267 us (level)
  matrix products: 22.1 us -> 10.7 us
  local copies, waits for them, and re-layouts: 17.8 us -> 28.2 us
  starting transfers between devices: 50.6 us -> 47.8 us
    unnamed x23 -> x35, local copies, waits for them, and re-layouts: 1.71 us -> 14.5 us
    dot_general x3 -> x2, matrix products: 13.9 us -> 6.52 us  [dot(): return jnp.dot(left, right, preferred_element_type=F32)]
    slice x2 -> x1, local copies, waits for them, and re-layouts: 4.17 us -> 0.03 us  [local(): up, down = both_ways(a[:, :cut], a[:, cut:])]
    dot_general x2, matrix products: 8.25 us -> 4.18 us  [dot_t(): lax.dot_general(left, right, (((1,), (1,)), ((), ())), preferred_element_...]
    all_gather x1, waiting for transfers between devices: 3.39 us -> 0.02 us  [local(): pieces = lax.all_gather(pieces, 'z', axis=0, tiled=True)]
    ppermute x30, waiting for transfers between devices: 140 us -> 143 us  [shift(): return lax.ppermute(v, axis, [(i, (i + by) % n) for i in range(n)])]
    ppermute x30, starting transfers between devices: 50.5 us -> 47.7 us  [shift(): return lax.ppermute(v, axis, [(i, (i + by) % n) for i in range(n)])]
    pallas_call x1 -> x2, Pallas kernels: 5.99 us -> 8.5 us  [product(): pl.pallas_call(kernel, grid=(steps,), in_specs=[pl.BlockSpec((m // steps,...]
  transfers between devices with their start and end apart: 33 -> 33, of which waited for: 25 -> 23; matrix products, arithmetic and copies ran while one was open for 15% -> 11% of each run, Pallas kernels for 2% -> 3%
where the time goes in v3:
time: 267 us; the launch traced here: 266 us
  waiting for transfers between devices  143 us (54%)
  starting transfers between devices  47.8 us (18%)
  local copies, waits for them, and re-layouts  28.2 us (11%)
  between operations  14.3 us (5%)
  other arithmetic  13.6 us (5%)
  matrix products  10.7 us (4%)
  Pallas kernels  8.5 us (3%)
    ppermute x30, waiting for transfers between devices, shift(): return lax.ppermute(v, axis, [(i, (i + by) % n) for i in range(n)])  143 us
    ppermute x30, starting transfers between devices, shift(): return lax.ppermute(v, axis, [(i, (i + by) % n) for i in range(n)])  47.7 us
    unnamed x35, local copies, waits for them, and re-layouts  14.5 us
    pallas_call x2, Pallas kernels, product(): pl.pallas_call(kernel, grid=(steps,), in_specs=[pl.BlockSpec((m // steps,...  8.5 us
    dot_general x2, matrix products, dot(): return jnp.dot(left, right, preferred_element_type=F32)  6.52 us
    dynamic_slice x4, local copies, waits for them, and re-layouts, part(): return lax.dynamic_slice_in_dim(v, index * size, size, dim)  6.31 us
    dynamic_update_slice x11, local copies, waits for them, and re-layouts, put(): lax.dynamic_update_slice(base, piece, (jnp.int32(row), jnp.int32(col)))  6.01 us
  transfers between devices with their start and end apart: 33, of which 23 were waited for; matrix products, arithmetic and copies ran while one was open for 11% of the time, Pallas kernels for 3%

profile of v3, /device:TPU:8, one launch (start us, length us, event | category | flops | bytes accessed | tf_op | source)
XLA Modules:
  0.0 266.5 jit_solution(16663951951768865262)
XLA Ops:
  14.9 3.1 %collective-permute-done = bf16[2,128,512]{2,1,0:T(8,128)(2,1)} collective-permute-done((bf16[2,128,512]{2,1,0:T(8,128)(2,1)S(1)}, bf16[2,128,512]{2,1,0:T(8,128)(2,1)}, u32[]{:S(2)}, u32[]{:S(2)}) %collective-permute-start) | collective-permute-done | bytes 262176 | tf_op jit(solution)/shard_map/ppermute | solution.py:16
  26.8 35.8 %collective-permute-done.1.got_ref = bf16[512,1792]{1,0:T(8,128)(2,1)S(1)} collective-permute-done((bf16[512,1792]{1,0:T(8,128)(2,1)}, bf16[512,1792]{1,0:T(8,128)(2,1)S(1)}, u32[]{:S(2)}, u32[]{:S(2)}) %collective-permute-start.1) | collective-permute-done | bytes 1835040 | tf_op jit(solution)/shard_map/ppermute | solution.py:16
  69.1 4.7 %shard_map.94 = bf16[1024,1792]{1,0:T(8,128)(2,1)S(1)} custom-call(bf16[1024,2048]{1,0:T(8,128)(2,1)S(1)} %copy-done.7, bf16[1024,1792]{1,0:T(8,128)(2,1)S(1)} %copy-done.2, bf16[512,1792]{1,0:T(8,128)(2,1)S(1)} %collective-permute-done.1.got_ref), custom_call_target="tpu_custom_call" | custom-call | flops 15000000512 | tf_op jit(solution)/shard_map/pallas_call | solution.py:54
  77.1 12.4 %collective-permute-done.3 = bf16[128,896]{1,0:T(8,128)(2,1)S(1)} collective-permute-done((bf16[128,896]{1,0:T(8,128)(2,1)}, bf16[128,896]{1,0:T(8,128)(2,1)S(1)}, u32[]{:S(2)}, u32[]{:S(2)}) %collective-permute-start.3) | collective-permute-done | bytes 229408 | tf_op jit(solution)/shard_map/ppermute | solution.py:16
  92.0 3.8 %shard_map.95 = bf16[1024,896]{1,0:T(8,128)(2,1)S(1)} custom-call(bf16[1024,2048]{1,0:T(8,128)(2,1)S(1)} %copy-done.8, bf16[896,512]{1,0:T(8,128)(2,1)S(1)} %get-tuple-element.60.kept_ref, bf16[896,512]{1,0:T(8,128)(2,1)} %collective-permute-done.2.got_ref), custom_call_target="tpu_custom_call" | custom-call | flops 40000000000 | tf_op jit(solution)/shard_map/pallas_call | solution.py:54
  97.9 4.1 %collective-permute-start.5 = (bf16[128,384]{1,0:T(8,128)(2,1)S(1)}, bf16[128,384]{1,0:T(8,128)(2,1)S(1)}, u32[]{:S(2)}, u32[]{:S(2)}) collective-permute-start(bf16[128,384]{1,0:T(8,128)(2,1)S(1)} %get-tuple-element.68), channel_id=1, source_target_pairs={{0,112},{16,0},{32,16},{48,32},{64,48},{80,64},{96,80},{112,96},{1... | collective-permute-start | bytes 294920 | tf_op jit(solution)/shard_map/ppermute | solution.py:16
  108.3 3.2 %collective-permute-start.7 = (bf16[128,896]{1,0:T(8,128)(2,1)S(1)}, bf16[128,896]{1,0:T(8,128)(2,1)S(1)}, u32[]{:S(2)}, u32[]{:S(2)}) collective-permute-start(bf16[128,896]{1,0:T(8,128)(2,1)S(1)} %get-tuple-element.73), channel_id=1, source_target_pairs={{0,112},{16,0},{32,16},{48,32},{64,48},{80,64},{96,80},{112,96},{1... | collective-permute-start | bytes 688136 | tf_op jit(solution)/shard_map/ppermute | solution.py:16
  111.5 10.1 %collective-permute-done.6 = bf16[128,896]{1,0:T(8,128)(2,1)S(1)} collective-permute-done((bf16[128,896]{1,0:T(8,128)(2,1)S(1)}, bf16[128,896]{1,0:T(8,128)(2,1)S(1)}, u32[]{:S(2)}, u32[]{:S(2)}) %collective-permute-start.6) | collective-permute-done | bytes 229408 | tf_op jit(solution)/shard_map/ppermute | solution.py:16
  126.1 9.9 %collective-permute-done.8 = bf16[128,896]{1,0:T(8,128)(2,1)S(1)} collective-permute-done((bf16[128,896]{1,0:T(8,128)(2,1)S(1)}, bf16[128,896]{1,0:T(8,128)(2,1)S(1)}, u32[]{:S(2)}, u32[]{:S(2)}) %collective-permute-start.8) | collective-permute-done | bytes 229408 | tf_op jit(solution)/shard_map/ppermute | solution.py:16
  140.6 4.0 %collective-permute-done.10 = bf16[128,896]{1,0:T(8,128)(2,1)S(1)} collective-permute-done((bf16[128,896]{1,0:T(8,128)(2,1)S(1)}, bf16[128,896]{1,0:T(8,128)(2,1)S(1)}, u32[]{:S(2)}, u32[]{:S(2)}) %collective-permute-start.10) | collective-permute-done | bytes 229408 | tf_op jit(solution)/shard_map/ppermute | solution.py:16
  153.8 5.3 %collective-permute-done.12 = bf16[128,896]{1,0:T(8,128)(2,1)S(1)} collective-permute-done((bf16[128,896]{1,0:T(8,128)(2,1)S(1)}, bf16[128,896]{1,0:T(8,128)(2,1)S(1)}, u32[]{:S(2)}, u32[]{:S(2)}) %collective-permute-start.12) | collective-permute-done | bytes 229408 | tf_op jit(solution)/shard_map/ppermute | solution.py:16
  164.8 9.4 %collective-permute-done.14 = bf16[128,896]{1,0:T(8,128)(2,1)S(1)} collective-permute-done((bf16[128,896]{1,0:T(8,128)(2,1)S(1)}, bf16[128,896]{1,0:T(8,128)(2,1)S(1)}, u32[]{:S(2)}, u32[]{:S(2)}) %collective-permute-start.14) | collective-permute-done | bytes 229408 | tf_op jit(solution)/shard_map/ppermute | solution.py:16
  180.1 8.7 %collective-permute-done.16 = bf16[128,896]{1,0:T(8,128)(2,1)S(1)} collective-permute-done((bf16[128,896]{1,0:T(8,128)(2,1)S(1)}, bf16[128,896]{1,0:T(8,128)(2,1)S(1)}, u32[]{:S(2)}, u32[]{:S(2)}) %collective-permute-start.16) | collective-permute-done | bytes 229408 | tf_op jit(solution)/shard_map/ppermute | solution.py:16
  188.9 3.2 %collective-permute-start.19 = (bf16[128,384]{1,0:T(8,128)(2,1)S(1)}, bf16[128,384]{1,0:T(8,128)(2,1)S(1)}, u32[]{:S(2)}, u32[]{:S(2)}) collective-permute-start(bf16[128,384]{1,0:T(8,128)(2,1)S(1)} %slice.131), channel_id=1, source_target_pairs={{0,112},{16,0},{32,16},{48,32},{64,48},{80,64},{96,80},{112,96},{1... | collective-permute-start | bytes 294920 | tf_op jit(solution)/shard_map/ppermute | solution.py:16
  193.6 4.3 %collective-permute-done.18 = bf16[128,512]{1,0:T(8,128)(2,1)S(1)} collective-permute-done((bf16[128,512]{1,0:T(8,128)(2,1)S(1)}, bf16[128,512]{1,0:T(8,128)(2,1)S(1)}, u32[]{:S(2)}, u32[]{:S(2)}) %collective-permute-start.18) | collective-permute-done | bytes 131104 | tf_op jit(solution)/shard_map/ppermute | solution.py:16
  199.2 3.5 %convolution_convert_fusion = bf16[512,1024]{1,0:T(8,128)(2,1)} fusion(bf16[896,1024]{1,0:T(8,128)(2,1)S(1)} %pad_maximum_fusion.1, bf16[1024,896]{1,0:T(8,128)(2,1)} %constant_dynamic-update-slice_fusion.9), kind=kOutput, calls=%fused_computation.6 | convolution fusion | flops 940048384 | bytes 3801088 | tf_op jit(solution)/shard_map/dot_general | solution.py:32
  205.6 3.0 %convert_add_fusion.1 = f32[512,1024]{1,0:T(8,128)S(1)} fusion(bf16[512,1024]{1,0:T(8,128)(2,1)S(1)} %collective-permute-done.20, bf16[896,1024]{1,0:T(8,128)(2,1)} %copy-done.9, bf16[1024,896]{1,0:T(8,128)(2,1)} %constant_dynamic-update-slice_fusion.9), kind=kOutput, calls=%fused_computation.1 | convolution fusion | flops 940572672 | bytes 5898240 | tf_op jit(solution)/shard_map/dot_general | solution.py:32
  215.8 2.9 %collective-permute-start.23 = (bf16[128,1024]{1,0:T(8,128)(2,1)S(1)}, bf16[128,1024]{1,0:T(8,128)(2,1)S(1)}, u32[]{:S(2)}, u32[]{:S(2)}) collective-permute-start(bf16[128,1024]{1,0:T(8,128)(2,1)S(1)} %get-tuple-element.105), channel_id=1, source_target_pairs={{0,6},{2,0},{4,2},{6,4},{1,7},{3,1},{5,3},{7,5},{8,14},{10,8},{12,... | collective-permute-start | bytes 786440 | tf_op jit(solution)/shard_map/ppermute | solution.py:16
  225.2 5.6 %collective-permute-done.23 = bf16[128,1024]{1,0:T(8,128)(2,1)S(1)} collective-permute-done((bf16[128,1024]{1,0:T(8,128)(2,1)S(1)}, bf16[128,1024]{1,0:T(8,128)(2,1)S(1)}, u32[]{:S(2)}, u32[]{:S(2)}) %collective-permute-start.23) | collective-permute-done | bytes 262176 | tf_op jit(solution)/shard_map/ppermute | solution.py:16
  230.8 3.9 %collective-permute-done.22 = bf16[128,1024]{1,0:T(8,128)(2,1)S(1)} collective-permute-done((bf16[128,1024]{1,0:T(8,128)(2,1)S(1)}, bf16[128,1024]{1,0:T(8,128)(2,1)S(1)}, u32[]{:S(2)}, u32[]{:S(2)}) %collective-permute-start.22) | collective-permute-done | bytes 262176 | tf_op jit(solution)/shard_map/ppermute | solution.py:16
  234.9 6.8 %collective-permute-done.27 = bf16[128,1024]{1,0:T(8,128)(2,1)S(1)} collective-permute-done((bf16[128,1024]{1,0:T(8,128)(2,1)S(1)}, bf16[128,1024]{1,0:T(8,128)(2,1)S(1)}, u32[]{:S(2)}, u32[]{:S(2)}) %collective-permute-start.27) | collective-permute-done | bytes 262176 | tf_op jit(solution)/shard_map/ppermute | solution.py:16
  241.7 3.4 %collective-permute-done.26 = bf16[128,1024]{1,0:T(8,128)(2,1)S(1)} collective-permute-done((bf16[128,1024]{1,0:T(8,128)(2,1)S(1)}, bf16[128,1024]{1,0:T(8,128)(2,1)S(1)}, u32[]{:S(2)}, u32[]{:S(2)}) %collective-permute-start.26) | collective-permute-done | bytes 262176 | tf_op jit(solution)/shard_map/ppermute | solution.py:16
  247.4 6.0 %collective-permute-done.28 = bf16[2,128,512]{2,1,0:T(8,128)(2,1)S(1)} collective-permute-done((bf16[2,128,512]{2,1,0:T(8,128)(2,1)S(1)}, bf16[2,128,512]{2,1,0:T(8,128)(2,1)S(1)}, u32[]{:S(2)}, u32[]{:S(2)}) %collective-permute-start.28) | collective-permute-done | bytes 262176 | tf_op jit(solution)/shard_map/ppermute | solution.py:16
  254.8 4.5 %collective-permute-done.29 = bf16[128,512]{1,0:T(8,128)(2,1)S(1)} collective-permute-done((bf16[128,512]{1,0:T(8,128)(2,1)S(1)}, bf16[128,512]{1,0:T(8,128)(2,1)S(1)}, u32[]{:S(2)}, u32[]{:S(2)}) %collective-permute-start.29) | collective-permute-done | bytes 131104 | tf_op jit(solution)/shard_map/ppermute | solution.py:16
  (136 shorter events, 90.5 us)
Async XLA Ops:
  7.2 57.7 %all-gather.3.cloned.1.call-start = ((), (), s32[]{:S(2)}) async-start(), calls=%async_computation.1 | async-start | bytes 4718592 | tf_op jit(solution)/shard_map/all_gather | solution.py:112
  8.2 9.7 %collective-permute-start = (bf16[2,128,512]{2,1,0:T(8,128)(2,1)S(1)}, bf16[2,128,512]{2,1,0:T(8,128)(2,1)}, u32[]{:S(2)}, u32[]{:S(2)}) collective-permute-start(bf16[2,128,512]{2,1,0:T(8,128)(2,1)S(1)} %pad_maximum_fusion.6), channel_id=1, source_target_pairs={{0,8},{8,0},{1,9},{9,1},{2,10},{10,2},{3,11},{11,3},{4,12},{12,4},... | collective-permute-start | bytes 786440 | tf_op jit(solution)/shard_map/ppermute | solution.py:16
  19.8 128.0 %reduce-scatter.2.cloned.1.call-start = ((), (), s32[]{:S(2)}) async-start(), calls=%async_computation.2 | async-start | bytes 4128768 | tf_op jit(solution)/shard_map/reduce_scatter | solution.py:128
  19.9 42.7 %collective-permute-start.1 = (bf16[512,1792]{1,0:T(8,128)(2,1)}, bf16[512,1792]{1,0:T(8,128)(2,1)S(1)}, u32[]{:S(2)}, u32[]{:S(2)}) collective-permute-start(bf16[512,1792]{1,0:T(8,128)(2,1)} %pad_maximum_fusion), channel_id=1, source_target_pairs={{0,8},{8,0},{1,9},{9,1},{2,10},{10,2},{3,11},{11,3},{4,12},{12,4},... | collective-permute-start | bytes 5505032 | tf_op jit(solution)/shard_map/ppermute | solution.py:16
  62.6 27.1 %collective-permute-start.2 = (bf16[896,512]{1,0:T(8,128)(2,1)}, bf16[896,512]{1,0:T(8,128)(2,1)}, u32[]{:S(2)}, u32[]{:S(2)}) collective-permute-start(bf16[896,512]{1,0:T(8,128)(2,1)} %get-tuple-element.61), channel_id=1, source_target_pairs={{0,8},{8,0},{1,9},{9,1},{2,10},{10,2},{3,11},{11,3},{4,12},{12,4},... | collective-permute-start | bytes 2752520 | tf_op jit(solution)/shard_map/ppermute | solution.py:16
  75.6 133.0 %all-gather.5.cloned.1.call-start = ((), (), s32[]{:S(2)}) async-start(), calls=%async_computation.3 | async-start | bytes 4128768 | tf_op jit(solution)/shard_map/all_gather | solution.py:159
  75.7 13.7 %collective-permute-start.3 = (bf16[128,896]{1,0:T(8,128)(2,1)}, bf16[128,896]{1,0:T(8,128)(2,1)S(1)}, u32[]{:S(2)}, u32[]{:S(2)}) collective-permute-start(bf16[128,896]{1,0:T(8,128)(2,1)} %get-tuple-element.63), channel_id=1, source_target_pairs={{0,8},{8,0},{1,9},{9,1},{2,10},{10,2},{3,11},{11,3},{4,12},{12,4},... | collective-permute-start | bytes 688136 | tf_op jit(solution)/shard_map/ppermute | solution.py:16
  95.9 12.2 %collective-permute-start.4 = (bf16[128,512]{1,0:T(8,128)(2,1)S(1)}, bf16[128,512]{1,0:T(8,128)(2,1)S(1)}, u32[]{:S(2)}, u32[]{:S(2)}) collective-permute-start(bf16[128,512]{1,0:T(8,128)(2,1)S(1)} %get-tuple-element.67), channel_id=1, source_target_pairs={{0,16},{16,32},{32,48},{48,64},{64,80},{80,96},{96,112},{112,0},{1... | collective-permute-start | bytes 393224 | tf_op jit(solution)/shard_map/ppermute | solution.py:16
  108.2 13.4 %collective-permute-start.6 = (bf16[128,896]{1,0:T(8,128)(2,1)S(1)}, bf16[128,896]{1,0:T(8,128)(2,1)S(1)}, u32[]{:S(2)}, u32[]{:S(2)}) collective-permute-start(bf16[128,896]{1,0:T(8,128)(2,1)S(1)} %get-tuple-element.72), channel_id=1, source_target_pairs={{0,16},{16,32},{32,48},{48,64},{64,80},{80,96},{96,112},{112,0},{1... | collective-permute-start | bytes 688136 | tf_op jit(solution)/shard_map/ppermute | solution.py:16
  108.3 13.3 %collective-permute-start.7 = (bf16[128,896]{1,0:T(8,128)(2,1)S(1)}, bf16[128,896]{1,0:T(8,128)(2,1)S(1)}, u32[]{:S(2)}, u32[]{:S(2)}) collective-permute-start(bf16[128,896]{1,0:T(8,128)(2,1)S(1)} %get-tuple-element.73), channel_id=1, source_target_pairs={{0,112},{16,0},{32,16},{48,32},{64,48},{80,64},{96,80},{112,96},{1... | collective-permute-start | bytes 688136 | tf_op jit(solution)/shard_map/ppermute | solution.py:16
  122.8 13.2 %collective-permute-start.8 = (bf16[128,896]{1,0:T(8,128)(2,1)S(1)}, bf16[128,896]{1,0:T(8,128)(2,1)S(1)}, u32[]{:S(2)}, u32[]{:S(2)}) collective-permute-start(bf16[128,896]{1,0:T(8,128)(2,1)S(1)} %get-tuple-element.76), channel_id=1, source_target_pairs={{0,16},{16,32},{32,48},{48,64},{64,80},{80,96},{96,112},{112,0},{1... | collective-permute-start | bytes 688136 | tf_op jit(solution)/shard_map/ppermute | solution.py:16
  124.4 11.7 %collective-permute-start.9 = (bf16[128,896]{1,0:T(8,128)(2,1)S(1)}, bf16[128,896]{1,0:T(8,128)(2,1)S(1)}, u32[]{:S(2)}, u32[]{:S(2)}) collective-permute-start(bf16[128,896]{1,0:T(8,128)(2,1)S(1)} %get-tuple-element.77), channel_id=1, source_target_pairs={{0,112},{16,0},{32,16},{48,32},{64,48},{80,64},{96,80},{112,96},{1... | collective-permute-start | bytes 688136 | tf_op jit(solution)/shard_map/ppermute | solution.py:16
  160.1 14.1 %collective-permute-start.14 = (bf16[128,896]{1,0:T(8,128)(2,1)S(1)}, bf16[128,896]{1,0:T(8,128)(2,1)S(1)}, u32[]{:S(2)}, u32[]{:S(2)}) collective-permute-start(bf16[128,896]{1,0:T(8,128)(2,1)S(1)} %collective-permute-done.12), channel_id=1, source_target_pairs={{0,16},{16,32},{32,48},{48,64},{64,80},{80,96},{96,112},{112,0},{1... | collective-permute-start | bytes 688136 | tf_op jit(solution)/shard_map/ppermute | solution.py:16
  162.1 13.4 %collective-permute-start.15 = (bf16[128,896]{1,0:T(8,128)(2,1)S(1)}, bf16[128,896]{1,0:T(8,128)(2,1)S(1)}, u32[]{:S(2)}, u32[]{:S(2)}) collective-permute-start(bf16[128,896]{1,0:T(8,128)(2,1)S(1)} %collective-permute-done.13), channel_id=1, source_target_pairs={{0,112},{16,0},{32,16},{48,32},{64,48},{80,64},{96,80},{112,96},{1... | collective-permute-start | bytes 688136 | tf_op jit(solution)/shard_map/ppermute | solution.py:16
  175.4 13.4 %collective-permute-start.16 = (bf16[128,896]{1,0:T(8,128)(2,1)S(1)}, bf16[128,896]{1,0:T(8,128)(2,1)S(1)}, u32[]{:S(2)}, u32[]{:S(2)}) collective-permute-start(bf16[128,896]{1,0:T(8,128)(2,1)S(1)} %collective-permute-done.14), channel_id=1, source_target_pairs={{0,16},{16,32},{32,48},{48,64},{64,80},{80,96},{96,112},{112,0},{1... | collective-permute-start | bytes 688136 | tf_op jit(solution)/shard_map/ppermute | solution.py:16
  176.5 12.3 %collective-permute-start.17 = (bf16[128,896]{1,0:T(8,128)(2,1)S(1)}, bf16[128,896]{1,0:T(8,128)(2,1)S(1)}, u32[]{:S(2)}, u32[]{:S(2)}) collective-permute-start(bf16[128,896]{1,0:T(8,128)(2,1)S(1)} %collective-permute-done.15), channel_id=1, source_target_pairs={{0,112},{16,0},{32,16},{48,32},{64,48},{80,64},{96,80},{112,96},{1... | collective-permute-start | bytes 688136 | tf_op jit(solution)/shard_map/ppermute | solution.py:16
  188.9 9.0 %collective-permute-start.18 = (bf16[128,512]{1,0:T(8,128)(2,1)S(1)}, bf16[128,512]{1,0:T(8,128)(2,1)S(1)}, u32[]{:S(2)}, u32[]{:S(2)}) collective-permute-start(bf16[128,512]{1,0:T(8,128)(2,1)S(1)} %slice.130), channel_id=1, source_target_pairs={{0,16},{16,32},{32,48},{48,64},{64,80},{80,96},{96,112},{112,0},{1... | collective-permute-start | bytes 393224 | tf_op jit(solution)/shard_map/ppermute | solution.py:16
  188.9 9.6 %collective-permute-start.19 = (bf16[128,384]{1,0:T(8,128)(2,1)S(1)}, bf16[128,384]{1,0:T(8,128)(2,1)S(1)}, u32[]{:S(2)}, u32[]{:S(2)}) collective-permute-start(bf16[128,384]{1,0:T(8,128)(2,1)S(1)} %slice.131), channel_id=1, source_target_pairs={{0,112},{16,0},{32,16},{48,32},{64,48},{80,64},{96,80},{112,96},{1... | collective-permute-start | bytes 294920 | tf_op jit(solution)/shard_map/ppermute | solution.py:16
  215.8 15.0 %collective-permute-start.23 = (bf16[128,1024]{1,0:T(8,128)(2,1)S(1)}, bf16[128,1024]{1,0:T(8,128)(2,1)S(1)}, u32[]{:S(2)}, u32[]{:S(2)}) collective-permute-start(bf16[128,1024]{1,0:T(8,128)(2,1)S(1)} %get-tuple-element.105), channel_id=1, source_target_pairs={{0,6},{2,0},{4,2},{6,4},{1,7},{3,1},{5,3},{7,5},{8,14},{10,8},{12,... | collective-permute-start | bytes 786440 | tf_op jit(solution)/shard_map/ppermute | solution.py:16
  218.7 16.0 %collective-permute-start.22 = (bf16[128,1024]{1,0:T(8,128)(2,1)S(1)}, bf16[128,1024]{1,0:T(8,128)(2,1)S(1)}, u32[]{:S(2)}, u32[]{:S(2)}) collective-permute-start(bf16[128,1024]{1,0:T(8,128)(2,1)S(1)} %get-tuple-element.104), channel_id=1, source_target_pairs={{0,2},{2,4},{4,6},{6,0},{1,3},{3,5},{5,7},{7,1},{8,10},{10,12},{12... | collective-permute-start | bytes 786440 | tf_op jit(solution)/shard_map/ppermute | solution.py:16
  218.7 16.0 %collective-permute-start.21 = (bf16[128,1024]{1,0:T(8,128)(2,1)S(1)}, bf16[128,1024]{1,0:T(8,128)(2,1)S(1)}, u32[]{:S(2)}, u32[]{:S(2)}) collective-permute-start(bf16[128,1024]{1,0:T(8,128)(2,1)S(1)} %get-tuple-element.103), channel_id=1, source_target_pairs={{0,4},{2,6},{4,0},{6,2},{1,5},{3,7},{5,1},{7,3},{8,12},{10,14},{12... | collective-permute-start | bytes 786440 | tf_op jit(solution)/shard_map/ppermute | solution.py:16
  223.1 18.6 %collective-permute-start.27 = (bf16[128,1024]{1,0:T(8,128)(2,1)S(1)}, bf16[128,1024]{1,0:T(8,128)(2,1)S(1)}, u32[]{:S(2)}, u32[]{:S(2)}) collective-permute-start(bf16[128,1024]{1,0:T(8,128)(2,1)S(1)} %get-tuple-element.112), channel_id=1, source_target_pairs={{0,6},{2,0},{4,2},{6,4},{1,7},{3,1},{5,3},{7,5},{8,14},{10,8},{12,... | collective-permute-start | bytes 786440 | tf_op jit(solution)/shard_map/ppermute | solution.py:16
  224.3 20.8 %collective-permute-start.26 = (bf16[128,1024]{1,0:T(8,128)(2,1)S(1)}, bf16[128,1024]{1,0:T(8,128)(2,1)S(1)}, u32[]{:S(2)}, u32[]{:S(2)}) collective-permute-start(bf16[128,1024]{1,0:T(8,128)(2,1)S(1)} %get-tuple-element.111), channel_id=1, source_target_pairs={{0,2},{2,4},{4,6},{6,0},{1,3},{3,5},{5,7},{7,1},{8,10},{10,12},{12... | collective-permute-start | bytes 786440 | tf_op jit(solution)/shard_map/ppermute | solution.py:16
  230.8 14.2 %collective-permute-start.25 = (bf16[128,1024]{1,0:T(8,128)(2,1)S(1)}, bf16[128,1024]{1,0:T(8,128)(2,1)S(1)}, u32[]{:S(2)}, u32[]{:S(2)}) collective-permute-start(bf16[128,1024]{1,0:T(8,128)(2,1)S(1)} %get-tuple-element.110), channel_id=1, source_target_pairs={{0,4},{2,6},{4,0},{6,2},{1,5},{3,7},{5,1},{7,3},{8,12},{10,14},{12... | collective-permute-start | bytes 786440 | tf_op jit(solution)/shard_map/ppermute | solution.py:16
  (26 other events, 212.3 us)
Sparse Core Ops, SparseCore 0:
  19.9 37.5 all-gather.2
  75.8 66.2 reduce-scatter.1
  147.9 59.5 all-gather.4

commit v4 on v3

--- a/solution.py
+++ b/solution.py
@@ -61,7 +61,7 @@
         ],
         out_specs=pl.BlockSpec((m // steps, width), lambda i: (i, 0)),
         out_shape=jax.ShapeDtypeStruct((m, width), BF16),
-        compiler_params=pltpu.CompilerParams(vmem_limit_bytes=32 << 20),
+        compiler_params=pltpu.CompilerParams(vmem_limit_bytes=60 << 20),
         cost_estimate=pl.CostEstimate(flops=flops, transcendentals=0, bytes_accessed=0),
     )(tokens, kept, got)
 
@@ -134,16 +134,13 @@
         jnp.concatenate([saved_got[:half], saved[:half], saved_got[half:], saved[half:]]),
     )
     down_got, saved, ready, w_got = join(down_got, saved, ready, w_got)
-    term = product(slope_kernel, tokens, 1, down_kept, down_got, cols, 2, int(4e10))
+    term = product(slope_kernel, tokens, 1, down_kept, down_got, cols, 2, int(45e9))
 
     def block(k):
         return part(term, owner(k), rows, 0)
 
     a = block(4)
-    up, down = both_ways(a[:, :cut], a[:, cut:])
-    down_pair = jnp.concatenate([down_kept, down_got], axis=1)
-    w_both = put(w_both, w_got, feats)
-    up, down, down_pair, w_both = join(up, down, down_pair, w_both)
+    up, down = join(*both_ways(a[:, :cut], a[:, cut:]))
     a, b = block(3), block(-3)
     up = jnp.concatenate([add(a[:, :cut], up), a[:, cut:]], axis=1)
     down = jnp.concatenate([b[:, :cut], add(b[:, cut:], down)], axis=1)
@@ -162,9 +159,18 @@
     both = both.astype(F32)
     hidden = (jax.nn.silu(both[:, :cols]) * both[:, cols:]).astype(BF16)
     spots = put(jnp.zeros((8 * rows, cols), BF16), hidden, place(0) * rows)
+    hidden, down_got, w_got = join(hidden, down_got, w_got)
     up, down = hidden, hidden
     for k in (1, 2, 3):
-        up, down = join(*both_ways(up, down))
+        up, down = both_ways(up, down)
+        if k == 1:
+            down_pair = jnp.concatenate([down_kept, down_got], axis=1)
+            up, down, down_pair, w_got = join(up, down, down_pair, w_got)
+        elif k == 2:
+            w_both = put(w_both, w_got, feats)
+            up, down, w_both = join(up, down, w_both)
+        else:
+            up, down = join(up, down)
         spots = put(put(spots, up, place(-k) * rows), down, place(k) * rows)
     up, down = both_ways(up[:, :cut], down[:, cut:])
     spots = put(put(spots, up, place(4) * rows), down, place(4) * rows, cut)

time: 267 us -> 267 us (level)
  local copies, waits for them, and re-layouts: 28.2 us -> 19.6 us
  waiting for transfers between devices: 143 us -> 149 us
  Pallas kernels: 8.5 us -> 13.4 us
    unnamed x35 -> x29, local copies, waits for them, and re-layouts: 14.5 us -> 3.55 us
    pallas_call x2, Pallas kernels: 8.5 us -> 13.4 us  [product(): pl.pallas_call(kernel, grid=(steps,), in_specs=[pl.BlockSpec((m // steps,...]
    all_gather x1, waiting for transfers between devices: 0.02 us -> 3.21 us  [local(): pieces = lax.all_gather(pieces, 'z', axis=0, tiled=True)]
  transfers between devices with their start and end apart: 33 -> 33, of which waited for: 23 -> 21; matrix products, arithmetic and copies ran while one was open for 11% -> 12% of each run, Pallas kernels for 3% -> 5%
where the time goes in v4:
time: 267 us; the launch traced here: 266 us
  waiting for transfers between devices  149 us (56%)
  starting transfers between devices  48 us (18%)
  local copies, waits for them, and re-layouts  19.6 us (7%)
  between operations  14.3 us (5%)
  Pallas kernels  13.4 us (5%)
  other arithmetic  12.9 us (5%)
  matrix products  9.75 us (4%)
    ppermute x30, waiting for transfers between devices, shift(): return lax.ppermute(v, axis, [(i, (i + by) % n) for i in range(n)])  145 us
    ppermute x30, starting transfers between devices, shift(): return lax.ppermute(v, axis, [(i, (i + by) % n) for i in range(n)])  47.9 us
    pallas_call x2, Pallas kernels, product(): pl.pallas_call(kernel, grid=(steps,), in_specs=[pl.BlockSpec((m // steps,...  13.4 us
    dynamic_update_slice x11, local copies, waits for them, and re-layouts, put(): lax.dynamic_update_slice(base, piece, (jnp.int32(row), jnp.int32(col)))  7.12 us
    dynamic_slice x4, local copies, waits for them, and re-layouts, part(): return lax.dynamic_slice_in_dim(v, index * size, size, dim)  6.48 us
    dot_general x2, matrix products, dot(): return jnp.dot(left, right, preferred_element_type=F32)  5.58 us
  transfers between devices with their start and end apart: 33, of which 21 were waited for; matrix products, arithmetic and copies ran while one was open for 12% of the time, Pallas kernels for 5%

profile of v4, /device:TPU:8, one launch (start us, length us, event | category | flops | bytes accessed | tf_op | source)
XLA Modules:
  0.0 266.5 jit_solution(12183673227621828103)
XLA Ops:
  27.0 34.4 %collective-permute-done.1.got_ref = bf16[512,1792]{1,0:T(8,128)(2,1)} collective-permute-done((bf16[512,1792]{1,0:T(8,128)(2,1)S(1)}, bf16[512,1792]{1,0:T(8,128)(2,1)}, u32[]{:S(2)}, u32[]{:S(2)}) %collective-permute-start.1) | collective-permute-done | bytes 1835040 | tf_op jit(solution)/shard_map/ppermute | solution.py:16
  65.0 8.1 %shard_map.94 = bf16[1024,1792]{1,0:T(8,128)(2,1)} custom-call(bf16[1024,2048]{1,0:T(8,128)(2,1)} %all-gather.3.cloned.1.call-done.left_ref, bf16[1024,1792]{1,0:T(8,128)(2,1)} %bitcast_dynamic-update-slice_fusion.kept_ref, bf16[512,1792]{1,0:T(8,128)(2,1)} %collective-permute-done.1.got_ref), custom_call_target="tpu_custom_call" | custom-call | flops 15000000512 | tf_op jit(solution)/shard_map/pallas_call | solution.py:54
  73.1 15.2 %collective-permute-done.3 = bf16[128,896]{1,0:T(8,128)(2,1)S(1)} collective-permute-done((bf16[128,896]{1,0:T(8,128)(2,1)S(1)}, bf16[128,896]{1,0:T(8,128)(2,1)S(1)}, u32[]{:S(2)}, u32[]{:S(2)}) %collective-permute-start.3) | collective-permute-done | bytes 229408 | tf_op jit(solution)/shard_map/ppermute | solution.py:16
  89.4 5.3 %shard_map.95 = bf16[1024,896]{1,0:T(8,128)(2,1)} custom-call(bf16[1024,2048]{1,0:T(8,128)(2,1)} %all-gather.3.cloned.1.call-done.left_ref, bf16[896,512]{1,0:T(8,128)(2,1)} %get-tuple-element.64.kept_ref, bf16[896,512]{1,0:T(8,128)(2,1)} %copy-done.11), custom_call_target="tpu_custom_call" | custom-call | flops 44999999488 | tf_op jit(solution)/shard_map/pallas_call | solution.py:54
  98.8 4.1 %collective-permute-start.5 = (bf16[128,384]{1,0:T(8,128)(2,1)S(1)}, bf16[128,384]{1,0:T(8,128)(2,1)S(1)}, u32[]{:S(2)}, u32[]{:S(2)}) collective-permute-start(bf16[128,384]{1,0:T(8,128)(2,1)S(1)} %get-tuple-element.72), channel_id=1, source_target_pairs={{0,112},{16,0},{32,16},{48,32},{64,48},{80,64},{96,80},{112,96},{1... | collective-permute-start | bytes 294920 | tf_op jit(solution)/shard_map/ppermute | solution.py:16
  102.9 4.4 %collective-permute-done.5 = bf16[128,384]{1,0:T(8,128)(2,1)S(1)} collective-permute-done((bf16[128,384]{1,0:T(8,128)(2,1)S(1)}, bf16[128,384]{1,0:T(8,128)(2,1)S(1)}, u32[]{:S(2)}, u32[]{:S(2)}) %collective-permute-start.5) | collective-permute-done | bytes 98336 | tf_op jit(solution)/shard_map/ppermute | solution.py:16
  111.0 3.2 %collective-permute-start.7 = (bf16[128,896]{1,0:T(8,128)(2,1)S(1)}, bf16[128,896]{1,0:T(8,128)(2,1)}, u32[]{:S(2)}, u32[]{:S(2)}) collective-permute-start(bf16[128,896]{1,0:T(8,128)(2,1)S(1)} %get-tuple-element.76), channel_id=1, source_target_pairs={{0,112},{16,0},{32,16},{48,32},{64,48},{80,64},{96,80},{112,96},{1... | collective-permute-start | bytes 688136 | tf_op jit(solution)/shard_map/ppermute | solution.py:16
  114.2 10.1 %collective-permute-done.6 = bf16[128,896]{1,0:T(8,128)(2,1)S(1)} collective-permute-done((bf16[128,896]{1,0:T(8,128)(2,1)S(1)}, bf16[128,896]{1,0:T(8,128)(2,1)S(1)}, u32[]{:S(2)}, u32[]{:S(2)}) %collective-permute-start.6) | collective-permute-done | bytes 229408 | tf_op jit(solution)/shard_map/ppermute | solution.py:16
  128.6 9.6 %collective-permute-done.8 = bf16[128,896]{1,0:T(8,128)(2,1)S(1)} collective-permute-done((bf16[128,896]{1,0:T(8,128)(2,1)S(1)}, bf16[128,896]{1,0:T(8,128)(2,1)S(1)}, u32[]{:S(2)}, u32[]{:S(2)}) %collective-permute-start.8) | collective-permute-done | bytes 229408 | tf_op jit(solution)/shard_map/ppermute | solution.py:16
  138.4 3.2 %collective-permute-start.11 = (bf16[128,896]{1,0:T(8,128)(2,1)S(1)}, bf16[128,896]{1,0:T(8,128)(2,1)}, u32[]{:S(2)}, u32[]{:S(2)}) collective-permute-start(bf16[128,896]{1,0:T(8,128)(2,1)S(1)} %get-tuple-element.84), channel_id=1, source_target_pairs={{0,112},{16,0},{32,16},{48,32},{64,48},{80,64},{96,80},{112,96},{1... | collective-permute-start | bytes 688136 | tf_op jit(solution)/shard_map/ppermute | solution.py:16
  141.7 4.0 %collective-permute-done.10 = bf16[128,896]{1,0:T(8,128)(2,1)S(1)} collective-permute-done((bf16[128,896]{1,0:T(8,128)(2,1)S(1)}, bf16[128,896]{1,0:T(8,128)(2,1)S(1)}, u32[]{:S(2)}, u32[]{:S(2)}) %collective-permute-start.10) | collective-permute-done | bytes 229408 | tf_op jit(solution)/shard_map/ppermute | solution.py:16
  149.4 3.4 %collective-permute-start.13 = (bf16[128,896]{1,0:T(8,128)(2,1)S(1)}, bf16[128,896]{1,0:T(8,128)(2,1)}, u32[]{:S(2)}, u32[]{:S(2)}) collective-permute-start(bf16[128,896]{1,0:T(8,128)(2,1)S(1)} %get-tuple-element.93), channel_id=1, source_target_pairs={{0,112},{16,0},{32,16},{48,32},{64,48},{80,64},{96,80},{112,96},{1... | collective-permute-start | bytes 688136 | tf_op jit(solution)/shard_map/ppermute | solution.py:16
  154.3 4.5 %collective-permute-done.12 = bf16[128,896]{1,0:T(8,128)(2,1)S(1)} collective-permute-done((bf16[128,896]{1,0:T(8,128)(2,1)S(1)}, bf16[128,896]{1,0:T(8,128)(2,1)S(1)}, u32[]{:S(2)}, u32[]{:S(2)}) %collective-permute-start.12) | collective-permute-done | bytes 229408 | tf_op jit(solution)/shard_map/ppermute | solution.py:16
  164.8 8.1 %collective-permute-done.14 = bf16[128,896]{1,0:T(8,128)(2,1)S(1)} collective-permute-done((bf16[128,896]{1,0:T(8,128)(2,1)S(1)}, bf16[128,896]{1,0:T(8,128)(2,1)S(1)}, u32[]{:S(2)}, u32[]{:S(2)}) %collective-permute-start.14) | collective-permute-done | bytes 229408 | tf_op jit(solution)/shard_map/ppermute | solution.py:16
  177.3 9.5 %collective-permute-done.16 = bf16[128,896]{1,0:T(8,128)(2,1)S(1)} collective-permute-done((bf16[128,896]{1,0:T(8,128)(2,1)S(1)}, bf16[128,896]{1,0:T(8,128)(2,1)S(1)}, u32[]{:S(2)}, u32[]{:S(2)}) %collective-permute-start.16) | collective-permute-done | bytes 229408 | tf_op jit(solution)/shard_map/ppermute | solution.py:16
  190.2 5.7 %collective-permute-done.18 = bf16[128,512]{1,0:T(8,128)(2,1)S(1)} collective-permute-done((bf16[128,512]{1,0:T(8,128)(2,1)S(1)}, bf16[128,512]{1,0:T(8,128)(2,1)S(1)}, u32[]{:S(2)}, u32[]{:S(2)}) %collective-permute-start.18) | collective-permute-done | bytes 131104 | tf_op jit(solution)/shard_map/ppermute | solution.py:16
  201.2 3.3 %convert_add_fusion.1 = f32[512,1024]{1,0:T(8,128)S(1)} fusion(bf16[512,1024]{1,0:T(8,128)(2,1)} %collective-permute-done.20, bf16[896,1024]{1,0:T(8,128)(2,1)} %copy-done.4, bf16[1024,896]{1,0:T(8,128)(2,1)} %copy-done.8), kind=kOutput, calls=%fused_computation.1 | convolution fusion | flops 940572672 | bytes 5898240 | tf_op jit(solution)/shard_map/dot_general | solution.py:32
  204.6 3.2 %all-gather.5.cloned.1.call-done = bf16[1024,1792]{1,0:T(8,128)(2,1)} async-done(((bf16[128,1792]{1,0:T(8,128)(2,1)}), bf16[1024,1792]{1,0:T(8,128)(2,1)}) %all-gather.5.cloned.1.call-update) | async-done | bytes 3670032 | tf_op jit(solution)/shard_map/all_gather | solution.py:156
  224.2 5.5 %collective-permute-done.23 = bf16[128,1024]{1,0:T(8,128)(2,1)S(1)} collective-permute-done((bf16[128,1024]{1,0:T(8,128)(2,1)S(1)}, bf16[128,1024]{1,0:T(8,128)(2,1)S(1)}, u32[]{:S(2)}, u32[]{:S(2)}) %collective-permute-start.23) | collective-permute-done | bytes 262176 | tf_op jit(solution)/shard_map/ppermute | solution.py:16
  229.7 3.9 %collective-permute-done.22 = bf16[128,1024]{1,0:T(8,128)(2,1)S(1)} collective-permute-done((bf16[128,1024]{1,0:T(8,128)(2,1)S(1)}, bf16[128,1024]{1,0:T(8,128)(2,1)S(1)}, u32[]{:S(2)}, u32[]{:S(2)}) %collective-permute-start.22) | collective-permute-done | bytes 262176 | tf_op jit(solution)/shard_map/ppermute | solution.py:16
  233.7 6.9 %collective-permute-done.27 = bf16[128,1024]{1,0:T(8,128)(2,1)S(1)} collective-permute-done((bf16[128,1024]{1,0:T(8,128)(2,1)S(1)}, bf16[128,1024]{1,0:T(8,128)(2,1)S(1)}, u32[]{:S(2)}, u32[]{:S(2)}) %collective-permute-start.27) | collective-permute-done | bytes 262176 | tf_op jit(solution)/shard_map/ppermute | solution.py:16
  240.7 3.4 %collective-permute-done.26 = bf16[128,1024]{1,0:T(8,128)(2,1)S(1)} collective-permute-done((bf16[128,1024]{1,0:T(8,128)(2,1)S(1)}, bf16[128,1024]{1,0:T(8,128)(2,1)S(1)}, u32[]{:S(2)}, u32[]{:S(2)}) %collective-permute-start.26) | collective-permute-done | bytes 262176 | tf_op jit(solution)/shard_map/ppermute | solution.py:16
  246.5 7.0 %collective-permute-done.28 = bf16[2,128,512]{2,1,0:T(8,128)(2,1)S(1)} collective-permute-done((bf16[2,128,512]{2,1,0:T(8,128)(2,1)S(1)}, bf16[2,128,512]{2,1,0:T(8,128)(2,1)S(1)}, u32[]{:S(2)}, u32[]{:S(2)}) %collective-permute-start.28) | collective-permute-done | bytes 262176 | tf_op jit(solution)/shard_map/ppermute | solution.py:16
  254.9 4.4 %collective-permute-done.29 = bf16[128,512]{1,0:T(8,128)(2,1)S(1)} collective-permute-done((bf16[128,512]{1,0:T(8,128)(2,1)S(1)}, bf16[128,512]{1,0:T(8,128)(2,1)S(1)}, u32[]{:S(2)}, u32[]{:S(2)}) %collective-permute-start.29) | collective-permute-done | bytes 131104 | tf_op jit(solution)/shard_map/ppermute | solution.py:16
  (130 shorter events, 81.9 us)
Async XLA Ops:
  7.2 57.8 %all-gather.3.cloned.1.call-start = ((), (), s32[]{:S(2)}) async-start(), calls=%async_computation.1 | async-start | bytes 4718592 | tf_op jit(solution)/shard_map/all_gather | solution.py:112
  8.2 9.6 %collective-permute-start = (bf16[2,128,512]{2,1,0:T(8,128)(2,1)S(1)}, bf16[2,128,512]{2,1,0:T(8,128)(2,1)S(1)}, u32[]{:S(2)}, u32[]{:S(2)}) collective-permute-start(bf16[2,128,512]{2,1,0:T(8,128)(2,1)S(1)} %pad_maximum_fusion.6), channel_id=1, source_target_pairs={{0,8},{8,0},{1,9},{9,1},{2,10},{10,2},{3,11},{11,3},{4,12},{12,4},... | collective-permute-start | bytes 786440 | tf_op jit(solution)/shard_map/ppermute | solution.py:16
  18.8 129.0 %reduce-scatter.2.cloned.1.call-start = ((), (), s32[]{:S(2)}) async-start(), calls=%async_computation.2 | async-start | bytes 4128768 | tf_op jit(solution)/shard_map/reduce_scatter | solution.py:128
  18.8 42.6 %collective-permute-start.1 = (bf16[512,1792]{1,0:T(8,128)(2,1)S(1)}, bf16[512,1792]{1,0:T(8,128)(2,1)}, u32[]{:S(2)}, u32[]{:S(2)}) collective-permute-start(bf16[512,1792]{1,0:T(8,128)(2,1)S(1)} %copy-done.5), channel_id=1, source_target_pairs={{0,8},{8,0},{1,9},{9,1},{2,10},{10,2},{3,11},{11,3},{4,12},{12,4},... | collective-permute-start | bytes 5505032 | tf_op jit(solution)/shard_map/ppermute | solution.py:16
  61.4 27.0 %collective-permute-start.2 = (bf16[896,512]{1,0:T(8,128)(2,1)}, bf16[896,512]{1,0:T(8,128)(2,1)S(1)}, u32[]{:S(2)}, u32[]{:S(2)}) collective-permute-start(bf16[896,512]{1,0:T(8,128)(2,1)} %get-tuple-element.65), channel_id=1, source_target_pairs={{0,8},{8,0},{1,9},{9,1},{2,10},{10,2},{3,11},{11,3},{4,12},{12,4},... | collective-permute-start | bytes 2752520 | tf_op jit(solution)/shard_map/ppermute | solution.py:16
  63.7 24.6 %collective-permute-start.3 = (bf16[128,896]{1,0:T(8,128)(2,1)S(1)}, bf16[128,896]{1,0:T(8,128)(2,1)S(1)}, u32[]{:S(2)}, u32[]{:S(2)}) collective-permute-start(bf16[128,896]{1,0:T(8,128)(2,1)S(1)} %get-tuple-element.67), channel_id=1, source_target_pairs={{0,8},{8,0},{1,9},{9,1},{2,10},{10,2},{3,11},{11,3},{4,12},{12,4},... | collective-permute-start | bytes 688136 | tf_op jit(solution)/shard_map/ppermute | solution.py:16
  73.0 134.7 %all-gather.5.cloned.1.call-start = ((), (), s32[]{:S(2)}) async-start(), calls=%async_computation.3 | async-start | bytes 4128768 | tf_op jit(solution)/shard_map/all_gather | solution.py:156
  96.8 12.1 %collective-permute-start.4 = (bf16[128,512]{1,0:T(8,128)(2,1)S(1)}, bf16[128,512]{1,0:T(8,128)(2,1)S(1)}, u32[]{:S(2)}, u32[]{:S(2)}) collective-permute-start(bf16[128,512]{1,0:T(8,128)(2,1)S(1)} %get-tuple-element.71), channel_id=1, source_target_pairs={{0,16},{16,32},{32,48},{48,64},{64,80},{80,96},{96,112},{112,0},{1... | collective-permute-start | bytes 393224 | tf_op jit(solution)/shard_map/ppermute | solution.py:16
  110.9 13.4 %collective-permute-start.6 = (bf16[128,896]{1,0:T(8,128)(2,1)S(1)}, bf16[128,896]{1,0:T(8,128)(2,1)S(1)}, u32[]{:S(2)}, u32[]{:S(2)}) collective-permute-start(bf16[128,896]{1,0:T(8,128)(2,1)S(1)} %get-tuple-element.75), channel_id=1, source_target_pairs={{0,16},{16,32},{32,48},{48,64},{64,80},{80,96},{96,112},{112,0},{1... | collective-permute-start | bytes 688136 | tf_op jit(solution)/shard_map/ppermute | solution.py:16
  111.0 13.3 %collective-permute-start.7 = (bf16[128,896]{1,0:T(8,128)(2,1)S(1)}, bf16[128,896]{1,0:T(8,128)(2,1)}, u32[]{:S(2)}, u32[]{:S(2)}) collective-permute-start(bf16[128,896]{1,0:T(8,128)(2,1)S(1)} %get-tuple-element.76), channel_id=1, source_target_pairs={{0,112},{16,0},{32,16},{48,32},{64,48},{80,64},{96,80},{112,96},{1... | collective-permute-start | bytes 688136 | tf_op jit(solution)/shard_map/ppermute | solution.py:16
  125.3 12.9 %collective-permute-start.8 = (bf16[128,896]{1,0:T(8,128)(2,1)S(1)}, bf16[128,896]{1,0:T(8,128)(2,1)S(1)}, u32[]{:S(2)}, u32[]{:S(2)}) collective-permute-start(bf16[128,896]{1,0:T(8,128)(2,1)S(1)} %get-tuple-element.79), channel_id=1, source_target_pairs={{0,16},{16,32},{32,48},{48,64},{64,80},{80,96},{96,112},{112,0},{1... | collective-permute-start | bytes 688136 | tf_op jit(solution)/shard_map/ppermute | solution.py:16
  127.0 11.2 %collective-permute-start.9 = (bf16[128,896]{1,0:T(8,128)(2,1)S(1)}, bf16[128,896]{1,0:T(8,128)(2,1)S(1)}, u32[]{:S(2)}, u32[]{:S(2)}) collective-permute-start(bf16[128,896]{1,0:T(8,128)(2,1)S(1)} %get-tuple-element.80), channel_id=1, source_target_pairs={{0,112},{16,0},{32,16},{48,32},{64,48},{80,64},{96,80},{112,96},{1... | collective-permute-start | bytes 688136 | tf_op jit(solution)/shard_map/ppermute | solution.py:16
  149.2 9.6 %collective-permute-start.12 = (bf16[128,896]{1,0:T(8,128)(2,1)S(1)}, bf16[128,896]{1,0:T(8,128)(2,1)S(1)}, u32[]{:S(2)}, u32[]{:S(2)}) collective-permute-start(bf16[128,896]{1,0:T(8,128)(2,1)S(1)} %get-tuple-element.93), channel_id=1, source_target_pairs={{0,16},{16,32},{32,48},{48,64},{64,80},{80,96},{96,112},{112,0},{1... | collective-permute-start | bytes 688136 | tf_op jit(solution)/shard_map/ppermute | solution.py:16
  149.4 9.5 %collective-permute-start.13 = (bf16[128,896]{1,0:T(8,128)(2,1)S(1)}, bf16[128,896]{1,0:T(8,128)(2,1)}, u32[]{:S(2)}, u32[]{:S(2)}) collective-permute-start(bf16[128,896]{1,0:T(8,128)(2,1)S(1)} %get-tuple-element.93), channel_id=1, source_target_pairs={{0,112},{16,0},{32,16},{48,32},{64,48},{80,64},{96,80},{112,96},{1... | collective-permute-start | bytes 688136 | tf_op jit(solution)/shard_map/ppermute | solution.py:16
  158.8 14.0 %collective-permute-start.14 = (bf16[128,896]{1,0:T(8,128)(2,1)S(1)}, bf16[128,896]{1,0:T(8,128)(2,1)S(1)}, u32[]{:S(2)}, u32[]{:S(2)}) collective-permute-start(bf16[128,896]{1,0:T(8,128)(2,1)S(1)} %collective-permute-done.12), channel_id=1, source_target_pairs={{0,16},{16,32},{32,48},{48,64},{64,80},{80,96},{96,112},{112,0},{1... | collective-permute-start | bytes 688136 | tf_op jit(solution)/shard_map/ppermute | solution.py:16
  161.0 13.1 %collective-permute-start.15 = (bf16[128,896]{1,0:T(8,128)(2,1)}, bf16[128,896]{1,0:T(8,128)(2,1)S(1)}, u32[]{:S(2)}, u32[]{:S(2)}) collective-permute-start(bf16[128,896]{1,0:T(8,128)(2,1)} %collective-permute-done.13), channel_id=1, source_target_pairs={{0,112},{16,0},{32,16},{48,32},{64,48},{80,64},{96,80},{112,96},{1... | collective-permute-start | bytes 688136 | tf_op jit(solution)/shard_map/ppermute | solution.py:16
  174.0 12.8 %collective-permute-start.16 = (bf16[128,896]{1,0:T(8,128)(2,1)S(1)}, bf16[128,896]{1,0:T(8,128)(2,1)S(1)}, u32[]{:S(2)}, u32[]{:S(2)}) collective-permute-start(bf16[128,896]{1,0:T(8,128)(2,1)S(1)} %collective-permute-done.14), channel_id=1, source_target_pairs={{0,16},{16,32},{32,48},{48,64},{64,80},{80,96},{96,112},{112,0},{1... | collective-permute-start | bytes 688136 | tf_op jit(solution)/shard_map/ppermute | solution.py:16
  175.5 11.3 %collective-permute-start.17 = (bf16[128,896]{1,0:T(8,128)(2,1)S(1)}, bf16[128,896]{1,0:T(8,128)(2,1)S(1)}, u32[]{:S(2)}, u32[]{:S(2)}) collective-permute-start(bf16[128,896]{1,0:T(8,128)(2,1)S(1)} %collective-permute-done.15), channel_id=1, source_target_pairs={{0,112},{16,0},{32,16},{48,32},{64,48},{80,64},{96,80},{112,96},{1... | collective-permute-start | bytes 688136 | tf_op jit(solution)/shard_map/ppermute | solution.py:16
  214.8 14.9 %collective-permute-start.23 = (bf16[128,1024]{1,0:T(8,128)(2,1)S(1)}, bf16[128,1024]{1,0:T(8,128)(2,1)S(1)}, u32[]{:S(2)}, u32[]{:S(2)}) collective-permute-start(bf16[128,1024]{1,0:T(8,128)(2,1)S(1)} %get-tuple-element.113), channel_id=1, source_target_pairs={{0,6},{2,0},{4,2},{6,4},{1,7},{3,1},{5,3},{7,5},{8,14},{10,8},{12,... | collective-permute-start | bytes 786440 | tf_op jit(solution)/shard_map/ppermute | solution.py:16
  217.6 16.0 %collective-permute-start.22 = (bf16[128,1024]{1,0:T(8,128)(2,1)S(1)}, bf16[128,1024]{1,0:T(8,128)(2,1)S(1)}, u32[]{:S(2)}, u32[]{:S(2)}) collective-permute-start(bf16[128,1024]{1,0:T(8,128)(2,1)S(1)} %get-tuple-element.112), channel_id=1, source_target_pairs={{0,2},{2,4},{4,6},{6,0},{1,3},{3,5},{5,7},{7,1},{8,10},{10,12},{12... | collective-permute-start | bytes 786440 | tf_op jit(solution)/shard_map/ppermute | solution.py:16
  217.6 16.0 %collective-permute-start.21 = (bf16[128,1024]{1,0:T(8,128)(2,1)S(1)}, bf16[128,1024]{1,0:T(8,128)(2,1)S(1)}, u32[]{:S(2)}, u32[]{:S(2)}) collective-permute-start(bf16[128,1024]{1,0:T(8,128)(2,1)S(1)} %get-tuple-element.111), channel_id=1, source_target_pairs={{0,4},{2,6},{4,0},{6,2},{1,5},{3,7},{5,1},{7,3},{8,12},{10,14},{12... | collective-permute-start | bytes 786440 | tf_op jit(solution)/shard_map/ppermute | solution.py:16
  222.1 18.6 %collective-permute-start.27 = (bf16[128,1024]{1,0:T(8,128)(2,1)S(1)}, bf16[128,1024]{1,0:T(8,128)(2,1)S(1)}, u32[]{:S(2)}, u32[]{:S(2)}) collective-permute-start(bf16[128,1024]{1,0:T(8,128)(2,1)S(1)} %get-tuple-element.120), channel_id=1, source_target_pairs={{0,6},{2,0},{4,2},{6,4},{1,7},{3,1},{5,3},{7,5},{8,14},{10,8},{12,... | collective-permute-start | bytes 786440 | tf_op jit(solution)/shard_map/ppermute | solution.py:16
  223.3 20.8 %collective-permute-start.26 = (bf16[128,1024]{1,0:T(8,128)(2,1)S(1)}, bf16[128,1024]{1,0:T(8,128)(2,1)S(1)}, u32[]{:S(2)}, u32[]{:S(2)}) collective-permute-start(bf16[128,1024]{1,0:T(8,128)(2,1)S(1)} %get-tuple-element.119), channel_id=1, source_target_pairs={{0,2},{2,4},{4,6},{6,0},{1,3},{3,5},{5,7},{7,1},{8,10},{10,12},{12... | collective-permute-start | bytes 786440 | tf_op jit(solution)/shard_map/ppermute | solution.py:16
  229.7 14.4 %collective-permute-start.25 = (bf16[128,1024]{1,0:T(8,128)(2,1)S(1)}, bf16[128,1024]{1,0:T(8,128)(2,1)S(1)}, u32[]{:S(2)}, u32[]{:S(2)}) collective-permute-start(bf16[128,1024]{1,0:T(8,128)(2,1)S(1)} %get-tuple-element.118), channel_id=1, source_target_pairs={{0,4},{2,6},{4,0},{6,2},{1,5},{3,7},{5,1},{7,3},{8,12},{10,14},{12... | collective-permute-start | bytes 786440 | tf_op jit(solution)/shard_map/ppermute | solution.py:16
  (23 other events, 205.8 us)
Sparse Core Ops, SparseCore 0:
  18.9 37.5 all-gather.2
  73.2 65.8 reduce-scatter.1
  147.9 59.8 all-gather.4

commit v5 on v3

--- a/solution.py
+++ b/solution.py
@@ -61,7 +61,7 @@
         ],
         out_specs=pl.BlockSpec((m // steps, width), lambda i: (i, 0)),
         out_shape=jax.ShapeDtypeStruct((m, width), BF16),
-        compiler_params=pltpu.CompilerParams(vmem_limit_bytes=32 << 20),
+        compiler_params=pltpu.CompilerParams(vmem_limit_bytes=60 << 20),
         cost_estimate=pl.CostEstimate(flops=flops, transcendentals=0, bytes_accessed=0),
     )(tokens, kept, got)
 

time: 267 us -> 266 us (level)
  local copies, waits for them, and re-layouts: 28.2 us -> 16.5 us
  Pallas kernels: 8.5 us -> 13.5 us
  waiting for transfers between devices: 143 us -> 147 us
    unnamed x35 -> x33, local copies, waits for them, and re-layouts: 14.5 us -> 5.35 us
    pallas_call x2, Pallas kernels: 8.5 us -> 13.5 us  [product(): pl.pallas_call(kernel, grid=(steps,), in_specs=[pl.BlockSpec((m // steps,...]
    dynamic_update_slice x11, local copies, waits for them, and re-layouts: 6.01 us -> 2.2 us  [put(): lax.dynamic_update_slice(base, piece, (jnp.int32(row), jnp.int32(col)))]
    all_gather x1, waiting for transfers between devices: 0.02 us -> 3.36 us  [local(): pieces = lax.all_gather(pieces, 'z', axis=0, tiled=True)]
  transfers between devices with their start and end apart: 33 -> 33, of which waited for: 23 -> 21; matrix products, arithmetic and copies ran while one was open for 11% -> 11% of each run, Pallas kernels for 3% -> 5%
where the time goes in v5:
time: 266 us; the launch traced here: 265 us
  waiting for transfers between devices  147 us (55%)
  starting transfers between devices  48.4 us (18%)
  local copies, waits for them, and re-layouts  16.5 us (6%)
  other arithmetic  15.8 us (6%)
  between operations  14.3 us (5%)
  Pallas kernels  13.5 us (5%)
  matrix products  9.56 us (4%)
    ppermute x30, waiting for transfers between devices, shift(): return lax.ppermute(v, axis, [(i, (i + by) % n) for i in range(n)])  143 us
    ppermute x30, starting transfers between devices, shift(): return lax.ppermute(v, axis, [(i, (i + by) % n) for i in range(n)])  48.3 us
    pallas_call x2, Pallas kernels, product(): pl.pallas_call(kernel, grid=(steps,), in_specs=[pl.BlockSpec((m // steps,...  13.5 us
    dynamic_slice x4, local copies, waits for them, and re-layouts, part(): return lax.dynamic_slice_in_dim(v, index * size, size, dim)  6.6 us
    dot_general x2, matrix products, dot(): return jnp.dot(left, right, preferred_element_type=F32)  5.39 us
    unnamed x33, local copies, waits for them, and re-layouts  5.35 us
  transfers between devices with their start and end apart: 33, of which 21 were waited for; matrix products, arithmetic and copies ran while one was open for 11% of the time, Pallas kernels for 5%

profile of v5, /device:TPU:8, one launch (start us, length us, event | category | flops | bytes accessed | tf_op | source)
XLA Modules:
  0.0 264.9 jit_solution(10608578705380761508)
XLA Ops:
  25.9 35.6 %collective-permute-done.1.got_ref = bf16[512,1792]{1,0:T(8,128)(2,1)S(1)} collective-permute-done((bf16[512,1792]{1,0:T(8,128)(2,1)}, bf16[512,1792]{1,0:T(8,128)(2,1)S(1)}, u32[]{:S(2)}, u32[]{:S(2)}) %collective-permute-start.1) | collective-permute-done | bytes 1835040 | tf_op jit(solution)/shard_map/ppermute | solution.py:16
  63.8 8.0 %shard_map.94 = bf16[1024,1792]{1,0:T(8,128)(2,1)} custom-call(bf16[1024,2048]{1,0:T(8,128)(2,1)} %all-gather.3.cloned.1.call-done.left_ref, bf16[1024,1792]{1,0:T(8,128)(2,1)} %copy-done, bf16[512,1792]{1,0:T(8,128)(2,1)} %copy-done.6), custom_call_target="tpu_custom_call" | custom-call | flops 15000000512 | tf_op jit(solution)/shard_map/pallas_call | solution.py:54
  73.4 15.1 %collective-permute-done.3 = bf16[128,896]{1,0:T(8,128)(2,1)S(1)} collective-permute-done((bf16[128,896]{1,0:T(8,128)(2,1)S(1)}, bf16[128,896]{1,0:T(8,128)(2,1)S(1)}, u32[]{:S(2)}, u32[]{:S(2)}) %collective-permute-start.3) | collective-permute-done | bytes 229408 | tf_op jit(solution)/shard_map/ppermute | solution.py:16
  88.6 5.5 %shard_map.95 = bf16[1024,896]{1,0:T(8,128)(2,1)} custom-call(bf16[1024,2048]{1,0:T(8,128)(2,1)} %all-gather.3.cloned.1.call-done.left_ref, bf16[896,512]{1,0:T(8,128)(2,1)} %get-tuple-element.60.kept_ref, bf16[896,512]{1,0:T(8,128)(2,1)} %collective-permute-done.2.got_ref), custom_call_target="tpu_custom_call" | custom-call | flops 40000000000 | tf_op jit(solution)/shard_map/pallas_call | solution.py:54
  98.1 4.0 %collective-permute-start.5 = (bf16[128,384]{1,0:T(8,128)(2,1)S(1)}, bf16[128,384]{1,0:T(8,128)(2,1)S(1)}, u32[]{:S(2)}, u32[]{:S(2)}) collective-permute-start(bf16[128,384]{1,0:T(8,128)(2,1)S(1)} %get-tuple-element.68), channel_id=1, source_target_pairs={{0,112},{16,0},{32,16},{48,32},{64,48},{80,64},{96,80},{112,96},{1... | collective-permute-start | bytes 294920 | tf_op jit(solution)/shard_map/ppermute | solution.py:16
  103.7 3.4 %pad_maximum_fusion.1 = bf16[896,1024]{1,0:T(8,128)(2,1)} fusion(bf16[896,512]{1,0:T(8,128)(2,1)} %collective-permute-done.2.got_ref, bf16[896,512]{1,0:T(8,128)(2,1)S(1)} %copy-done.4), kind=kLoop, calls=%fused_computation.3 | loop fusion | flops 3670016 | bytes 3670016 | tf_op jit(solution)/shard_map/concatenate | solution.py:144
  110.2 3.2 %collective-permute-start.7 = (bf16[128,896]{1,0:T(8,128)(2,1)S(1)}, bf16[128,896]{1,0:T(8,128)(2,1)S(1)}, u32[]{:S(2)}, u32[]{:S(2)}) collective-permute-start(bf16[128,896]{1,0:T(8,128)(2,1)S(1)} %get-tuple-element.73), channel_id=1, source_target_pairs={{0,112},{16,0},{32,16},{48,32},{64,48},{80,64},{96,80},{112,96},{1... | collective-permute-start | bytes 688136 | tf_op jit(solution)/shard_map/ppermute | solution.py:16
  113.4 10.1 %collective-permute-done.6 = bf16[128,896]{1,0:T(8,128)(2,1)S(1)} collective-permute-done((bf16[128,896]{1,0:T(8,128)(2,1)S(1)}, bf16[128,896]{1,0:T(8,128)(2,1)S(1)}, u32[]{:S(2)}, u32[]{:S(2)}) %collective-permute-start.6) | collective-permute-done | bytes 229408 | tf_op jit(solution)/shard_map/ppermute | solution.py:16
  128.0 7.8 %collective-permute-done.8 = bf16[128,896]{1,0:T(8,128)(2,1)S(1)} collective-permute-done((bf16[128,896]{1,0:T(8,128)(2,1)S(1)}, bf16[128,896]{1,0:T(8,128)(2,1)S(1)}, u32[]{:S(2)}, u32[]{:S(2)}) %collective-permute-start.8) | collective-permute-done | bytes 229408 | tf_op jit(solution)/shard_map/ppermute | solution.py:16
  137.1 3.2 %collective-permute-start.11 = (bf16[128,896]{1,0:T(8,128)(2,1)S(1)}, bf16[128,896]{1,0:T(8,128)(2,1)S(1)}, u32[]{:S(2)}, u32[]{:S(2)}) collective-permute-start(bf16[128,896]{1,0:T(8,128)(2,1)S(1)} %get-tuple-element.81), channel_id=1, source_target_pairs={{0,112},{16,0},{32,16},{48,32},{64,48},{80,64},{96,80},{112,96},{1... | collective-permute-start | bytes 688136 | tf_op jit(solution)/shard_map/ppermute | solution.py:16
  140.3 4.0 %collective-permute-done.10 = bf16[128,896]{1,0:T(8,128)(2,1)S(1)} collective-permute-done((bf16[128,896]{1,0:T(8,128)(2,1)S(1)}, bf16[128,896]{1,0:T(8,128)(2,1)S(1)}, u32[]{:S(2)}, u32[]{:S(2)}) %collective-permute-start.10) | collective-permute-done | bytes 229408 | tf_op jit(solution)/shard_map/ppermute | solution.py:16
  148.1 3.1 %collective-permute-start.13 = (bf16[128,896]{1,0:T(8,128)(2,1)S(1)}, bf16[128,896]{1,0:T(8,128)(2,1)S(1)}, u32[]{:S(2)}, u32[]{:S(2)}) collective-permute-start(bf16[128,896]{1,0:T(8,128)(2,1)S(1)} %get-tuple-element.88), channel_id=1, source_target_pairs={{0,112},{16,0},{32,16},{48,32},{64,48},{80,64},{96,80},{112,96},{1... | collective-permute-start | bytes 688136 | tf_op jit(solution)/shard_map/ppermute | solution.py:16
  151.2 5.0 %collective-permute-done.12 = bf16[128,896]{1,0:T(8,128)(2,1)S(1)} collective-permute-done((bf16[128,896]{1,0:T(8,128)(2,1)S(1)}, bf16[128,896]{1,0:T(8,128)(2,1)S(1)}, u32[]{:S(2)}, u32[]{:S(2)}) %collective-permute-start.12) | collective-permute-done | bytes 229408 | tf_op jit(solution)/shard_map/ppermute | solution.py:16
  160.0 11.0 %collective-permute-done.14 = bf16[128,896]{1,0:T(8,128)(2,1)S(1)} collective-permute-done((bf16[128,896]{1,0:T(8,128)(2,1)S(1)}, bf16[128,896]{1,0:T(8,128)(2,1)S(1)}, u32[]{:S(2)}, u32[]{:S(2)}) %collective-permute-start.14) | collective-permute-done | bytes 229408 | tf_op jit(solution)/shard_map/ppermute | solution.py:16
  175.4 9.8 %collective-permute-done.16 = bf16[128,896]{1,0:T(8,128)(2,1)S(1)} collective-permute-done((bf16[128,896]{1,0:T(8,128)(2,1)S(1)}, bf16[128,896]{1,0:T(8,128)(2,1)S(1)}, u32[]{:S(2)}, u32[]{:S(2)}) %collective-permute-start.16) | collective-permute-done | bytes 229408 | tf_op jit(solution)/shard_map/ppermute | solution.py:16
  188.8 5.7 %collective-permute-done.18 = bf16[128,512]{1,0:T(8,128)(2,1)S(1)} collective-permute-done((bf16[128,512]{1,0:T(8,128)(2,1)S(1)}, bf16[128,512]{1,0:T(8,128)(2,1)S(1)}, u32[]{:S(2)}, u32[]{:S(2)}) %collective-permute-start.18) | collective-permute-done | bytes 131104 | tf_op jit(solution)/shard_map/ppermute | solution.py:16
  199.7 3.1 %convert_add_fusion.1 = f32[512,1024]{1,0:T(8,128)S(1)} fusion(bf16[512,1024]{1,0:T(8,128)(2,1)S(1)} %collective-permute-done.20, bf16[896,1024]{1,0:T(8,128)(2,1)} %pad_maximum_fusion.1, bf16[1024,896]{1,0:T(8,128)(2,1)} %copy-done.9), kind=kOutput, calls=%fused_computation.1 | convolution fusion | flops 940572672 | bytes 5898240 | tf_op jit(solution)/shard_map/dot_general | solution.py:32
  202.8 3.4 %all-gather.5.cloned.1.call-done = bf16[1024,1792]{1,0:T(8,128)(2,1)} async-done(((bf16[128,1792]{1,0:T(8,128)(2,1)}), bf16[1024,1792]{1,0:T(8,128)(2,1)}) %all-gather.5.cloned.1.call-update) | async-done | bytes 3670032 | tf_op jit(solution)/shard_map/all_gather | solution.py:159
  222.5 5.5 %collective-permute-done.23 = bf16[128,1024]{1,0:T(8,128)(2,1)S(1)} collective-permute-done((bf16[128,1024]{1,0:T(8,128)(2,1)S(1)}, bf16[128,1024]{1,0:T(8,128)(2,1)S(1)}, u32[]{:S(2)}, u32[]{:S(2)}) %collective-permute-start.23) | collective-permute-done | bytes 262176 | tf_op jit(solution)/shard_map/ppermute | solution.py:16
  228.1 3.9 %collective-permute-done.22 = bf16[128,1024]{1,0:T(8,128)(2,1)S(1)} collective-permute-done((bf16[128,1024]{1,0:T(8,128)(2,1)S(1)}, bf16[128,1024]{1,0:T(8,128)(2,1)S(1)}, u32[]{:S(2)}, u32[]{:S(2)}) %collective-permute-start.22) | collective-permute-done | bytes 262176 | tf_op jit(solution)/shard_map/ppermute | solution.py:16
  232.1 6.9 %collective-permute-done.27 = bf16[128,1024]{1,0:T(8,128)(2,1)S(1)} collective-permute-done((bf16[128,1024]{1,0:T(8,128)(2,1)S(1)}, bf16[128,1024]{1,0:T(8,128)(2,1)S(1)}, u32[]{:S(2)}, u32[]{:S(2)}) %collective-permute-start.27) | collective-permute-done | bytes 262176 | tf_op jit(solution)/shard_map/ppermute | solution.py:16
  239.1 3.4 %collective-permute-done.26 = bf16[128,1024]{1,0:T(8,128)(2,1)S(1)} collective-permute-done((bf16[128,1024]{1,0:T(8,128)(2,1)S(1)}, bf16[128,1024]{1,0:T(8,128)(2,1)S(1)}, u32[]{:S(2)}, u32[]{:S(2)}) %collective-permute-start.26) | collective-permute-done | bytes 262176 | tf_op jit(solution)/shard_map/ppermute | solution.py:16
  244.9 7.0 %collective-permute-done.28 = bf16[2,128,512]{2,1,0:T(8,128)(2,1)S(1)} collective-permute-done((bf16[2,128,512]{2,1,0:T(8,128)(2,1)S(1)}, bf16[2,128,512]{2,1,0:T(8,128)(2,1)S(1)}, u32[]{:S(2)}, u32[]{:S(2)}) %collective-permute-start.28) | collective-permute-done | bytes 262176 | tf_op jit(solution)/shard_map/ppermute | solution.py:16
  253.3 4.4 %collective-permute-done.29 = bf16[128,512]{1,0:T(8,128)(2,1)S(1)} collective-permute-done((bf16[128,512]{1,0:T(8,128)(2,1)S(1)}, bf16[128,512]{1,0:T(8,128)(2,1)S(1)}, u32[]{:S(2)}, u32[]{:S(2)}) %collective-permute-start.29) | collective-permute-done | bytes 131104 | tf_op jit(solution)/shard_map/ppermute | solution.py:16
  (134 shorter events, 78.5 us)
Async XLA Ops:
  7.2 56.6 %all-gather.3.cloned.1.call-start = ((), (), s32[]{:S(2)}) async-start(), calls=%async_computation.1 | async-start | bytes 4718592 | tf_op jit(solution)/shard_map/all_gather | solution.py:112
  8.2 9.6 %collective-permute-start = (bf16[2,128,512]{2,1,0:T(8,128)(2,1)S(1)}, bf16[2,128,512]{2,1,0:T(8,128)(2,1)S(1)}, u32[]{:S(2)}, u32[]{:S(2)}) collective-permute-start(bf16[2,128,512]{2,1,0:T(8,128)(2,1)S(1)} %pad_maximum_fusion.6), channel_id=1, source_target_pairs={{0,8},{8,0},{1,9},{9,1},{2,10},{10,2},{3,11},{11,3},{4,12},{12,4},... | collective-permute-start | bytes 786440 | tf_op jit(solution)/shard_map/ppermute | solution.py:16
  18.8 127.6 %reduce-scatter.2.cloned.1.call-start = ((), (), s32[]{:S(2)}) async-start(), calls=%async_computation.2 | async-start | bytes 4128768 | tf_op jit(solution)/shard_map/reduce_scatter | solution.py:128
  18.8 42.7 %collective-permute-start.1 = (bf16[512,1792]{1,0:T(8,128)(2,1)}, bf16[512,1792]{1,0:T(8,128)(2,1)S(1)}, u32[]{:S(2)}, u32[]{:S(2)}) collective-permute-start(bf16[512,1792]{1,0:T(8,128)(2,1)} %pad_maximum_fusion), channel_id=1, source_target_pairs={{0,8},{8,0},{1,9},{9,1},{2,10},{10,2},{3,11},{11,3},{4,12},{12,4},... | collective-permute-start | bytes 5505032 | tf_op jit(solution)/shard_map/ppermute | solution.py:16
  61.5 27.1 %collective-permute-start.2 = (bf16[896,512]{1,0:T(8,128)(2,1)}, bf16[896,512]{1,0:T(8,128)(2,1)}, u32[]{:S(2)}, u32[]{:S(2)}) collective-permute-start(bf16[896,512]{1,0:T(8,128)(2,1)} %get-tuple-element.61), channel_id=1, source_target_pairs={{0,8},{8,0},{1,9},{9,1},{2,10},{10,2},{3,11},{11,3},{4,12},{12,4},... | collective-permute-start | bytes 2752520 | tf_op jit(solution)/shard_map/ppermute | solution.py:16
  71.9 134.3 %all-gather.5.cloned.1.call-start = ((), (), s32[]{:S(2)}) async-start(), calls=%async_computation.3 | async-start | bytes 4128768 | tf_op jit(solution)/shard_map/all_gather | solution.py:159
  72.0 16.5 %collective-permute-start.3 = (bf16[128,896]{1,0:T(8,128)(2,1)S(1)}, bf16[128,896]{1,0:T(8,128)(2,1)S(1)}, u32[]{:S(2)}, u32[]{:S(2)}) collective-permute-start(bf16[128,896]{1,0:T(8,128)(2,1)S(1)} %get-tuple-element.63), channel_id=1, source_target_pairs={{0,8},{8,0},{1,9},{9,1},{2,10},{10,2},{3,11},{11,3},{4,12},{12,4},... | collective-permute-start | bytes 688136 | tf_op jit(solution)/shard_map/ppermute | solution.py:16
  96.0 12.2 %collective-permute-start.4 = (bf16[128,512]{1,0:T(8,128)(2,1)S(1)}, bf16[128,512]{1,0:T(8,128)(2,1)S(1)}, u32[]{:S(2)}, u32[]{:S(2)}) collective-permute-start(bf16[128,512]{1,0:T(8,128)(2,1)S(1)} %get-tuple-element.67), channel_id=1, source_target_pairs={{0,16},{16,32},{32,48},{48,64},{64,80},{80,96},{96,112},{112,0},{1... | collective-permute-start | bytes 393224 | tf_op jit(solution)/shard_map/ppermute | solution.py:16
  110.1 13.4 %collective-permute-start.6 = (bf16[128,896]{1,0:T(8,128)(2,1)S(1)}, bf16[128,896]{1,0:T(8,128)(2,1)S(1)}, u32[]{:S(2)}, u32[]{:S(2)}) collective-permute-start(bf16[128,896]{1,0:T(8,128)(2,1)S(1)} %get-tuple-element.72), channel_id=1, source_target_pairs={{0,16},{16,32},{32,48},{48,64},{64,80},{80,96},{96,112},{112,0},{1... | collective-permute-start | bytes 688136 | tf_op jit(solution)/shard_map/ppermute | solution.py:16
  110.2 13.4 %collective-permute-start.7 = (bf16[128,896]{1,0:T(8,128)(2,1)S(1)}, bf16[128,896]{1,0:T(8,128)(2,1)S(1)}, u32[]{:S(2)}, u32[]{:S(2)}) collective-permute-start(bf16[128,896]{1,0:T(8,128)(2,1)S(1)} %get-tuple-element.73), channel_id=1, source_target_pairs={{0,112},{16,0},{32,16},{48,32},{64,48},{80,64},{96,80},{112,96},{1... | collective-permute-start | bytes 688136 | tf_op jit(solution)/shard_map/ppermute | solution.py:16
  124.7 11.1 %collective-permute-start.8 = (bf16[128,896]{1,0:T(8,128)(2,1)S(1)}, bf16[128,896]{1,0:T(8,128)(2,1)S(1)}, u32[]{:S(2)}, u32[]{:S(2)}) collective-permute-start(bf16[128,896]{1,0:T(8,128)(2,1)S(1)} %get-tuple-element.76), channel_id=1, source_target_pairs={{0,16},{16,32},{32,48},{48,64},{64,80},{80,96},{96,112},{112,0},{1... | collective-permute-start | bytes 688136 | tf_op jit(solution)/shard_map/ppermute | solution.py:16
  126.3 9.5 %collective-permute-start.9 = (bf16[128,896]{1,0:T(8,128)(2,1)S(1)}, bf16[128,896]{1,0:T(8,128)(2,1)S(1)}, u32[]{:S(2)}, u32[]{:S(2)}) collective-permute-start(bf16[128,896]{1,0:T(8,128)(2,1)S(1)} %get-tuple-element.77), channel_id=1, source_target_pairs={{0,112},{16,0},{32,16},{48,32},{64,48},{80,64},{96,80},{112,96},{1... | collective-permute-start | bytes 688136 | tf_op jit(solution)/shard_map/ppermute | solution.py:16
  156.3 14.7 %collective-permute-start.14 = (bf16[128,896]{1,0:T(8,128)(2,1)S(1)}, bf16[128,896]{1,0:T(8,128)(2,1)S(1)}, u32[]{:S(2)}, u32[]{:S(2)}) collective-permute-start(bf16[128,896]{1,0:T(8,128)(2,1)S(1)} %collective-permute-done.12), channel_id=1, source_target_pairs={{0,16},{16,32},{32,48},{48,64},{64,80},{80,96},{96,112},{112,0},{1... | collective-permute-start | bytes 688136 | tf_op jit(solution)/shard_map/ppermute | solution.py:16
  158.4 13.7 %collective-permute-start.15 = (bf16[128,896]{1,0:T(8,128)(2,1)S(1)}, bf16[128,896]{1,0:T(8,128)(2,1)S(1)}, u32[]{:S(2)}, u32[]{:S(2)}) collective-permute-start(bf16[128,896]{1,0:T(8,128)(2,1)S(1)} %collective-permute-done.13), channel_id=1, source_target_pairs={{0,112},{16,0},{32,16},{48,32},{64,48},{80,64},{96,80},{112,96},{1... | collective-permute-start | bytes 688136 | tf_op jit(solution)/shard_map/ppermute | solution.py:16
  172.1 13.1 %collective-permute-start.16 = (bf16[128,896]{1,0:T(8,128)(2,1)S(1)}, bf16[128,896]{1,0:T(8,128)(2,1)S(1)}, u32[]{:S(2)}, u32[]{:S(2)}) collective-permute-start(bf16[128,896]{1,0:T(8,128)(2,1)S(1)} %collective-permute-done.14), channel_id=1, source_target_pairs={{0,16},{16,32},{32,48},{48,64},{64,80},{80,96},{96,112},{112,0},{1... | collective-permute-start | bytes 688136 | tf_op jit(solution)/shard_map/ppermute | solution.py:16
  174.0 11.3 %collective-permute-start.17 = (bf16[128,896]{1,0:T(8,128)(2,1)S(1)}, bf16[128,896]{1,0:T(8,128)(2,1)S(1)}, u32[]{:S(2)}, u32[]{:S(2)}) collective-permute-start(bf16[128,896]{1,0:T(8,128)(2,1)S(1)} %collective-permute-done.15), channel_id=1, source_target_pairs={{0,112},{16,0},{32,16},{48,32},{64,48},{80,64},{96,80},{112,96},{1... | collective-permute-start | bytes 688136 | tf_op jit(solution)/shard_map/ppermute | solution.py:16
  185.4 9.0 %collective-permute-start.18 = (bf16[128,512]{1,0:T(8,128)(2,1)S(1)}, bf16[128,512]{1,0:T(8,128)(2,1)S(1)}, u32[]{:S(2)}, u32[]{:S(2)}) collective-permute-start(bf16[128,512]{1,0:T(8,128)(2,1)S(1)} %slice.130), channel_id=1, source_target_pairs={{0,16},{16,32},{32,48},{48,64},{64,80},{80,96},{96,112},{112,0},{1... | collective-permute-start | bytes 393224 | tf_op jit(solution)/shard_map/ppermute | solution.py:16
  213.2 14.9 %collective-permute-start.23 = (bf16[128,1024]{1,0:T(8,128)(2,1)S(1)}, bf16[128,1024]{1,0:T(8,128)(2,1)S(1)}, u32[]{:S(2)}, u32[]{:S(2)}) collective-permute-start(bf16[128,1024]{1,0:T(8,128)(2,1)S(1)} %get-tuple-element.105), channel_id=1, source_target_pairs={{0,6},{2,0},{4,2},{6,4},{1,7},{3,1},{5,3},{7,5},{8,14},{10,8},{12,... | collective-permute-start | bytes 786440 | tf_op jit(solution)/shard_map/ppermute | solution.py:16
  216.0 16.0 %collective-permute-start.22 = (bf16[128,1024]{1,0:T(8,128)(2,1)S(1)}, bf16[128,1024]{1,0:T(8,128)(2,1)S(1)}, u32[]{:S(2)}, u32[]{:S(2)}) collective-permute-start(bf16[128,1024]{1,0:T(8,128)(2,1)S(1)} %get-tuple-element.104), channel_id=1, source_target_pairs={{0,2},{2,4},{4,6},{6,0},{1,3},{3,5},{5,7},{7,1},{8,10},{10,12},{12... | collective-permute-start | bytes 786440 | tf_op jit(solution)/shard_map/ppermute | solution.py:16
  216.0 16.0 %collective-permute-start.21 = (bf16[128,1024]{1,0:T(8,128)(2,1)S(1)}, bf16[128,1024]{1,0:T(8,128)(2,1)S(1)}, u32[]{:S(2)}, u32[]{:S(2)}) collective-permute-start(bf16[128,1024]{1,0:T(8,128)(2,1)S(1)} %get-tuple-element.103), channel_id=1, source_target_pairs={{0,4},{2,6},{4,0},{6,2},{1,5},{3,7},{5,1},{7,3},{8,12},{10,14},{12... | collective-permute-start | bytes 786440 | tf_op jit(solution)/shard_map/ppermute | solution.py:16
  220.4 18.6 %collective-permute-start.27 = (bf16[128,1024]{1,0:T(8,128)(2,1)S(1)}, bf16[128,1024]{1,0:T(8,128)(2,1)S(1)}, u32[]{:S(2)}, u32[]{:S(2)}) collective-permute-start(bf16[128,1024]{1,0:T(8,128)(2,1)S(1)} %get-tuple-element.112), channel_id=1, source_target_pairs={{0,6},{2,0},{4,2},{6,4},{1,7},{3,1},{5,3},{7,5},{8,14},{10,8},{12,... | collective-permute-start | bytes 786440 | tf_op jit(solution)/shard_map/ppermute | solution.py:16
  221.7 20.8 %collective-permute-start.26 = (bf16[128,1024]{1,0:T(8,128)(2,1)S(1)}, bf16[128,1024]{1,0:T(8,128)(2,1)S(1)}, u32[]{:S(2)}, u32[]{:S(2)}) collective-permute-start(bf16[128,1024]{1,0:T(8,128)(2,1)S(1)} %get-tuple-element.111), channel_id=1, source_target_pairs={{0,2},{2,4},{4,6},{6,0},{1,3},{3,5},{5,7},{7,1},{8,10},{10,12},{12... | collective-permute-start | bytes 786440 | tf_op jit(solution)/shard_map/ppermute | solution.py:16
  228.1 14.4 %collective-permute-start.25 = (bf16[128,1024]{1,0:T(8,128)(2,1)S(1)}, bf16[128,1024]{1,0:T(8,128)(2,1)S(1)}, u32[]{:S(2)}, u32[]{:S(2)}) collective-permute-start(bf16[128,1024]{1,0:T(8,128)(2,1)S(1)} %get-tuple-element.110), channel_id=1, source_target_pairs={{0,4},{2,6},{4,0},{6,2},{1,5},{3,7},{5,1},{7,3},{8,12},{10,14},{12... | collective-permute-start | bytes 786440 | tf_op jit(solution)/shard_map/ppermute | solution.py:16
  242.7 9.2 %collective-permute-start.28 = (bf16[2,128,512]{2,1,0:T(8,128)(2,1)S(1)}, bf16[2,128,512]{2,1,0:T(8,128)(2,1)S(1)}, u32[]{:S(2)}, u32[]{:S(2)}) collective-permute-start(bf16[2,128,512]{2,1,0:T(8,128)(2,1)S(1)} %pad_maximum_fusion.7), channel_id=1, source_target_pairs={{0,8},{8,0},{1,9},{9,1},{2,10},{10,2},{3,11},{11,3},{4,12},{12,4},... | collective-permute-start | bytes 786440 | tf_op jit(solution)/shard_map/ppermute | solution.py:16
  (25 other events, 183.9 us)
Sparse Core Ops, SparseCore 0:
  18.9 37.5 all-gather.2
  72.0 63.8 reduce-scatter.1
  146.5 59.6 all-gather.4
